TPU v7x, 32 devices: a whole 2x2x4 slice. The times are simulated.
32 devices in a mesh: fsdp: 32 (over z, y, x, core).
Axes of the slice: x: 2, y: 2, z: 4, core: 2. Of those that a mesh axis runs over, the one named last changes fastest.
Arguments:
- tokens: bfloat16 [32768, 1024], P('fsdp'), may hold values from -5 to 5
- cotangent: bfloat16 [32768, 1024], P('fsdp'), may hold values from -6 to 6
- segment: int32 [32768], P('fsdp'), may hold values from -1 to 511, as said below
- w_qkv: bfloat16 [3072, 1024], P('fsdp'), may hold values from -0.09375 to 0.09375
- w_attn_out: bfloat16 [1024, 1024], P('fsdp'), may hold values from -0.75 to 0.75
- w_in: bfloat16 [5248, 1024], P('fsdp'), may hold values from -0.1875 to 0.1875
- w_ff_out: bfloat16 [1024, 2624], P('fsdp'), may hold values from -0.125 to 0.125
- norm_one: bfloat16 [1024], P('fsdp'), may hold values from 0.25 to 1.75
- norm_two: bfloat16 [1024], P('fsdp'), may hold values from 0.25 to 1.75
Outputs:
- output: bfloat16 [32768, 1024], P('fsdp')
- grad_tokens: float32 [32768, 1024], P('fsdp')
- grad_qkv: float32 [3072, 1024], P('fsdp')
- grad_attn_out: float32 [1024, 1024], P('fsdp')
- grad_in: float32 [5248, 1024], P('fsdp')
- grad_ff_out: float32 [1024, 2624], P('fsdp')
- grad_norm_one: float32 [1024], P('fsdp')
- grad_norm_two: float32 [1024], P('fsdp')
Inputs may be any that keep to these rules, and one draw needn't show every extreme that they name: `segment`: within each block of 1024 slots the non-negative values start at 0 and rise by one at each new sequence, and the -1 slots, if any, come last; each run of one value other than -1 is at most 1024 long and at least 2 long unless -1 slots follow it; some run is exactly 1024 long, and some block reaches the largest value.
All inputs are finite; a program needn't handle non-finite values.
Results may differ from a plain program's by a relative error of at most 0.0084.
Values may be sent and summed in bfloat16 or wider, within the bound.
No kernel may reach another device: no remote copies, remote signals or barrier semaphores. Data moves between devices by JAX's collectives and lax.ppermute only.
A program may use at most 320 MiB of HBM per device.

v0:
```python
import math

import jax
import jax.numpy as jnp
from jax import lax
from jax.sharding import PartitionSpec as P

HD = 64


EPS = 1e-05
THETA = 160000.0


def matmul_nt(left, right):
    return lax.dot_general(
        left, right, (((1,), (1,)), ((), ())), preferred_element_type=jnp.float32
    )


def matmul_tn(left, right):
    return lax.dot_general(
        left, right, (((0,), (0,)), ((), ())), preferred_element_type=jnp.float32
    )


def heads_first(flat):
    return flat.reshape(flat.shape[0], -1, HD).transpose(1, 0, 2)


def heads_last(split):
    return split.transpose(1, 0, 2).reshape(split.shape[1], -1)


def rotate(field):
    half = field.shape[-1] // 2
    return jnp.concatenate([-field[..., half:], field[..., :half]], axis=-1)


def unrotate(field):
    half = field.shape[-1] // 2
    return jnp.concatenate([field[..., half:], -field[..., :half]], axis=-1)


def rope_tables(segment):
    count = segment.shape[0]
    slots = jnp.arange(count, dtype=jnp.int32)
    begins = jnp.concatenate([jnp.ones((1,), dtype=jnp.bool_), segment[1:] != segment[:-1]])
    starts = lax.cummax(jnp.where(begins, slots, 0), axis=0)
    positions = (slots - starts).astype(jnp.float32)
    half = HD // 2
    freqs = THETA ** (-2.0 * jnp.arange(half, dtype=jnp.float32) / HD)
    angles = positions[:, None] * freqs[None, :]
    cosine = jnp.concatenate([jnp.cos(angles), jnp.cos(angles)], axis=1)[None]
    sine = jnp.concatenate([jnp.sin(angles), jnp.sin(angles)], axis=1)[None]
    same = (segment[:, None] == segment[None, :]) & (segment[:, None] >= 0)
    allowed = same | (slots[:, None] == slots[None, :])
    return (cosine, sine, allowed)


def layer_norm(field):
    centre = jnp.mean(field, axis=-1, keepdims=True)
    centered = field - centre
    variance = jnp.mean(centered * centered, axis=-1, keepdims=True)
    inverse = lax.rsqrt(variance + EPS)
    return (centered * inverse, inverse)


def norm_backward(grad_normed, normed, inverse, gain):
    grad_hat = grad_normed * gain.astype(jnp.float32)
    first = jnp.mean(grad_hat, axis=-1, keepdims=True)
    second = jnp.mean(grad_hat * normed, axis=-1, keepdims=True)
    return (inverse * (grad_hat - first - normed * second), jnp.sum(grad_normed * normed, axis=0))


def gelu_parts(pre):
    cdf = 0.5 * (1.0 + lax.erf(pre * 0.7071067811865476))
    density = jnp.exp(-0.5 * pre * pre) * 0.3989422804014327
    return (pre * cdf, cdf + pre * density)


def attend_forward(query_rot, key_rot, value_all, allowed):
    scale = 1.0 / math.sqrt(HD)

    def per_head(operands):
        query_head, key_head, value_head = operands
        scores = matmul_nt(query_head, key_head) * scale
        scores = jnp.where(allowed, scores, -1e30)
        top_score = jnp.max(scores, axis=1, keepdims=True)
        totals = jnp.sum(jnp.exp(scores - top_score), axis=1, keepdims=True)
        log_total = top_score + jnp.log(totals)
        weights = jnp.exp(scores - log_total).astype(jnp.bfloat16)
        result = jnp.dot(weights, value_head, preferred_element_type=jnp.float32)
        return (result.astype(jnp.bfloat16), log_total[:, 0])

    return lax.map(per_head, (query_rot, key_rot, value_all))


def attend_backward(query_rot, key_rot, value_all, head_out, grad_heads, log_totals, allowed):
    scale = 1.0 / math.sqrt(HD)

    def per_head(operands):
        query_head, key_head, value_head, out_head, grad_head, log_head = operands
        scores = matmul_nt(query_head, key_head) * scale
        scores = jnp.where(allowed, scores, -1e30)
        weights = jnp.where(allowed, jnp.exp(scores - log_head[:, None]), 0.0)
        grad_value = matmul_tn(weights.astype(jnp.bfloat16), grad_head)
        grad_weights = matmul_nt(grad_head, value_head)
        delta = jnp.sum(
            grad_head.astype(jnp.float32) * out_head.astype(jnp.float32), axis=1, keepdims=True
        )
        grad_scores = (weights * (grad_weights - delta)).astype(jnp.bfloat16)
        grad_query = jnp.dot(grad_scores, key_head, preferred_element_type=jnp.float32) * scale
        grad_key = matmul_tn(grad_scores, query_head) * scale
        return (grad_query, grad_key, grad_value)

    return lax.map(per_head, (query_rot, key_rot, value_all, head_out, grad_heads, log_totals))


def forward_part(tokens, segment, w_qkv, w_attn_out, w_in, w_ff_out, norm_one, norm_two):
    width = tokens.shape[1]
    hidden_units = w_ff_out.shape[1]
    cosine, sine, allowed = rope_tables(segment)
    resid_in = tokens.astype(jnp.float32)
    normed_one, inverse_one = layer_norm(resid_in)
    hidden_one = (normed_one * norm_one.astype(jnp.float32)).astype(jnp.bfloat16)
    projected = matmul_nt(hidden_one, w_qkv)
    query_all = heads_first(projected[:, :width])
    key_all = heads_first(projected[:, width : 2 * width])
    value_all = heads_first(projected[:, 2 * width :]).astype(jnp.bfloat16)
    query_rot = (query_all * cosine + rotate(query_all) * sine).astype(jnp.bfloat16)
    key_rot = (key_all * cosine + rotate(key_all) * sine).astype(jnp.bfloat16)
    head_out, log_totals = attend_forward(query_rot, key_rot, value_all, allowed)
    attn_out = heads_last(head_out)
    resid_mid = resid_in + matmul_nt(attn_out, w_attn_out)
    normed_two, inverse_two = layer_norm(resid_mid)
    hidden_two = (normed_two * norm_two.astype(jnp.float32)).astype(jnp.bfloat16)
    inner = matmul_nt(hidden_two, w_in)
    gelu_value, gelu_slope = gelu_parts(inner[:, :hidden_units])
    gate_half = inner[:, hidden_units:]
    mixed = (gelu_value * gate_half).astype(jnp.bfloat16)
    output = (resid_mid + matmul_nt(mixed, w_ff_out)).astype(jnp.bfloat16)
    saved = (
        cosine,
        sine,
        allowed,
        normed_one,
        inverse_one,
        hidden_one,
        query_rot,
        key_rot,
        value_all,
        head_out,
        log_totals,
        attn_out,
        normed_two,
        inverse_two,
        hidden_two,
        gelu_value,
        gelu_slope,
        gate_half,
        mixed,
    )
    return (output, saved)


def ffn_backward(cotangent, saved, w_in, w_ff_out, norm_two):
    normed_two, inverse_two, hidden_two = (saved[12], saved[13], saved[14])
    gelu_value, gelu_slope, gate_half, mixed = (saved[15], saved[16], saved[17], saved[18])
    grad_ff_out = matmul_tn(cotangent, mixed)
    grad_mixed = jnp.dot(cotangent, w_ff_out, preferred_element_type=jnp.float32)
    grad_inner = jnp.concatenate(
        [grad_mixed * gate_half * gelu_slope, grad_mixed * gelu_value], axis=1
    ).astype(jnp.bfloat16)
    grad_in = matmul_tn(grad_inner, hidden_two)
    grad_hidden_two = jnp.dot(grad_inner, w_in, preferred_element_type=jnp.float32)
    grad_mid_norm, grad_norm_two = norm_backward(grad_hidden_two, normed_two, inverse_two, norm_two)
    grad_mid = cotangent.astype(jnp.float32) + grad_mid_norm
    return (grad_in, grad_ff_out, grad_norm_two, grad_mid)


def attn_backward(grad_mid, saved, w_qkv, w_attn_out, norm_one):
    cosine, sine, allowed, normed_one, inverse_one, hidden_one = saved[:6]
    query_rot, key_rot, value_all, head_out, log_totals, attn_out = saved[6:12]
    grad_mid_low = grad_mid.astype(jnp.bfloat16)
    grad_attn_out = matmul_tn(grad_mid_low, attn_out)
    grad_heads = heads_first(
        jnp.dot(grad_mid_low, w_attn_out, preferred_element_type=jnp.float32).astype(jnp.bfloat16)
    )
    grad_query, grad_key, grad_value = attend_backward(
        query_rot, key_rot, value_all, head_out, grad_heads, log_totals, allowed
    )
    grad_query = grad_query * cosine + unrotate(grad_query * sine)
    grad_key = grad_key * cosine + unrotate(grad_key * sine)
    grad_projected = jnp.concatenate(
        [heads_last(grad_query), heads_last(grad_key), heads_last(grad_value)], axis=1
    ).astype(jnp.bfloat16)
    grad_qkv = matmul_tn(grad_projected, hidden_one)
    grad_hidden_one = jnp.dot(grad_projected, w_qkv, preferred_element_type=jnp.float32)
    grad_in_norm, grad_norm_one = norm_backward(grad_hidden_one, normed_one, inverse_one, norm_one)
    grad_tokens = grad_mid + grad_in_norm
    return (grad_qkv, grad_attn_out, grad_norm_one, grad_tokens)


def body(tokens, cotangent, segment, w_qkv, w_attn_out, w_in, w_ff_out, norm_one, norm_two):
    full_qkv, full_attn_out, full_in, full_ff_out, full_one, full_two = (
        lax.all_gather(w_qkv, "fsdp", axis=0, tiled=True),
        lax.all_gather(w_attn_out, "fsdp", axis=0, tiled=True),
        lax.all_gather(w_in, "fsdp", axis=0, tiled=True),
        lax.all_gather(w_ff_out, "fsdp", axis=0, tiled=True),
        lax.all_gather(norm_one, "fsdp", axis=0, tiled=True),
        lax.all_gather(norm_two, "fsdp", axis=0, tiled=True),
    )
    output, saved = forward_part(
        tokens, segment, full_qkv, full_attn_out, full_in, full_ff_out, full_one, full_two
    )
    back_qkv, back_attn_out, back_in, back_ff_out, back_one, back_two = (
        lax.all_gather(w_qkv, "fsdp", axis=0, tiled=True),
        lax.all_gather(w_attn_out, "fsdp", axis=0, tiled=True),
        lax.all_gather(w_in, "fsdp", axis=0, tiled=True),
        lax.all_gather(w_ff_out, "fsdp", axis=0, tiled=True),
        lax.all_gather(norm_one, "fsdp", axis=0, tiled=True),
        lax.all_gather(norm_two, "fsdp", axis=0, tiled=True),
    )
    grad_in, grad_ff_out, grad_two, grad_mid = ffn_backward(
        cotangent, saved, back_in, back_ff_out, back_two
    )
    grad_qkv, grad_attn_out, grad_one, grad_tokens = attn_backward(
        grad_mid, saved, back_qkv, back_attn_out, back_one
    )
    shard_qkv, shard_attn_out, shard_in, shard_ff_out, shard_one, shard_two = (
        lax.psum_scatter(grad_qkv, "fsdp", scatter_dimension=0, tiled=True),
        lax.psum_scatter(grad_attn_out, "fsdp", scatter_dimension=0, tiled=True),
        lax.psum_scatter(grad_in, "fsdp", scatter_dimension=0, tiled=True),
        lax.psum_scatter(grad_ff_out, "fsdp", scatter_dimension=0, tiled=True),
        lax.psum_scatter(grad_one, "fsdp", scatter_dimension=0, tiled=True),
        lax.psum_scatter(grad_two, "fsdp", scatter_dimension=0, tiled=True),
    )
    return (
        output,
        grad_tokens,
        shard_qkv,
        shard_attn_out,
        shard_in,
        shard_ff_out,
        shard_one,
        shard_two,
    )


def solution(mesh):
    return jax.shard_map(
        body,
        mesh=mesh,
        in_specs=(
            P("fsdp", None),
            P("fsdp", None),
            P("fsdp"),
            P("fsdp", None),
            P("fsdp", None),
            P("fsdp", None),
            P("fsdp", None),
            P("fsdp"),
            P("fsdp"),
        ),
        out_specs=(
            P("fsdp", None),
            P("fsdp", None),
            P("fsdp", None),
            P("fsdp", None),
            P("fsdp", None),
            P("fsdp", None),
            P("fsdp"),
            P("fsdp"),
        ),
        check_vma=False,
    )
```

profile of v0, /device:TPU:0, one launch (start us, length us, event | category | flops | bytes accessed | tf_op | source)
XLA Modules:
  0.0 1062.2 jit_solution(13721867878056923128)
XLA Ops:
  16.0 42.4 %all-reduce.7 = (bf16[1024]{0:T(1024)(128)(2,1)S(1)}, bf16[1024]{0:T(1024)(128)(2,1)S(1)}) all-reduce(bf16[1024]{0:T(1024)(128)(2,1)S(1)} %dynamic-update-slice, bf16[1024]{0:T(1024)(128)(2,1)S(1)} %dynamic-update-slice.1), channel_id=1, replica_groups=mesh['fsdp'=32] {'fsdp'}, use_global_device_ids=true, to_apply=%add | all-reduce | flops 2048 | bytes 8192
  63.8 19.6 %all-gather.6.cloned.1.call-done = bf16[3072,1024]{1,0:T(8,128)(2,1)} async-done(((bf16[96,1024]{1,0:T(8,128)(2,1)}), bf16[3072,1024]{1,0:T(8,128)(2,1)}) %all-gather.6.cloned.1.call-update) | async-done | bytes 6291472 | tf_op jit(solution)/shard_map/all_gather | solution.py:207
  83.3 9.3 fusion.85
  98.6 5.3 copy.54
  103.9 5.3 copy.55
  109.3 4.7 slice_negate_fusion.2
  119.1 4.7 copy.57
  123.9 4.8 copy.58
  132.6 4.8 copy.59
  137.4 86.2 %while.28 = (s32[]{:T(128)}, bf16[16,1024,64]{1,2,0:T(8,128)(2,1)}, f32[16,1024]{1,0:T(8,128)S(1)}, bf16[16,1024,64]{2,1,0:T(8,128)(2,1)}, bf16[16,1024,64]{2,1,...) while((s32[]{:T(128)}, bf16[16,1024,64]{1,2,0:T(8,128)(2,1)}, ...), condition=%wide.region_7.8_spmd.clone, body=%wide.region_4.7_spmd.clone.sunk | while | flops 280034304 | bytes 13548649 | solution.py:96
  223.7 4.8 fusion.97
  231.8 13.8 %reshape.169 = bf16[5248,1024]{1,0:T(8,128)(2,1)} reshape(bf16[32,164,1024]{2,1,0:T(8,128)(2,1)} %all-gather.12.cloned.1.call-done) | data formatting | bytes 21495808
  245.6 20.9 %fusion.92 = f32[1024,5248]{1,0:T(8,128)} fusion(bf16[5248,1024]{1,0:T(8,128)(2,1)} %reshape.169, f32[1024,1024]{0,1:T(8,128)} %copy-done.7, f32[1024]{0:T(1024)S(1)} %convert_element_type.83, f32[1024]{0:T(1024)S(1)} %add_rsqrt_fusion, f32[1024]{0:T(1024)S(1)} %broadcast_multiply_fusion.6), kind=kOutput, calls=%fused_computation.148 | convolution fusion | flops 11010048000 | bytes 36450304 | tf_op jit(solution)/shard_map/dot_general | solution.py:16
  266.6 32.5 %all-gather.10.cloned.1.call-done = bf16[1024,2624]{1,0:T(8,128)(2,1)} async-done(((bf16[32,2624]{1,0:T(8,128)(2,1)}), bf16[1024,2624]{1,0:T(8,128)(2,1)}) %all-gather.10.cloned.1.call-update) | async-done | bytes 5373968 | tf_op jit(solution)/shard_map/all_gather | solution.py:210
  299.1 20.6 %fusion.57 = (bf16[1024,2624]{1,0:T(8,128)(2,1)}, bf16[1024,2624]{1,0:T(8,128)(2,1)}, bf16[1024,2624]{1,0:T(8,128)(2,1)}) fusion(f32[1024,5248]{1,0:T(8,128)} %fusion.92, bf16[1024,1024]{1,0:T(8,128)(2,1)} %param.14, bf16[1024,2624]{1,0:T(8,128)(2,1)} %all-gather.10.cloned.1.call-done), kind=kOutput, calls=%fused_computation.64 | convolution fusion | flops 5545918464 | bytes 45088768 | tf_op jit(solution)/shard_map/dot_general | solution.py:171
  319.7 26.3 %multiply_reduce_fusion = (f32[1024]{0:T(1024)S(1)}, f32[1024]{0:T(1024)S(1)}, f32[1024]{0:T(1024)S(1)}, f32[1024,1024]{0,1:T(8,128)}) fusion(f32[1024,1024]{0,1:T(8,128)S(1)} %copy-done.8, f32[1024]{0:T(1024)S(1)} %add_rsqrt_fusion, f32[1024]{0:T(1024)S(1)} %broadcast_multiply_fusion.6, f32[1024]{0:T(1024)S(1)} %convert_element_type.83, ...), kind=kOutput, calls=%fused_computation.101 | convolution fusion | flops 11035735040 | bytes 29908992 | tf_op jit(solution)/shard_map/dot_general | solution.py:176
  357.0 5.2 convolution_convert_fusion
  365.4 11.3 %convolution_bitcast_fusion = f32[1024,2624]{0,1:T(8,128)} fusion(bf16[1024,2624]{1,0:T(8,128)(2,1)} %get-tuple-element.296, bf16[1024,1024]{1,0:T(8,128)(2,1)} %param.14), kind=kOutput, calls=%fused_computation.72 | convolution fusion | flops 5502926848 | bytes 18219008 | tf_op jit(solution)/shard_map/dot_general | solution.py:22
  376.6 12.0 %copy.74 = f32[1024,2624]{1,0:T(8,128)} copy(f32[1024,2624]{0,1:T(8,128)} %convolution_bitcast_fusion) | data formatting | bytes 21495808
  389.1 272.5 %while.29 = (s32[]{:T(128)}, f32[16,1024,64]{1,2,0:T(8,128)}, f32[16,1024,64]{1,2,0:T(8,128)}, bf16[16,1024,64]{1,2,0:T(8,128)(2,1)}, bf16[16,1024,64]{2,1,0:T(8...) while((s32[]{:T(128)}, f32[16,1024,64]{1,2,0:T(8,128)}, ...), condition=%wide.region_14.15_spmd.clone, body=%wide.region_12.14_spmd.clone.sunk | while | flops 684063744 | bytes 39094436 | solution.py:117
  389.1 4.7 exponential_select_fusion.2
  507.8 4.7 exponential_select_fusion.2
  593.2 4.6 exponential_select_fusion.2
  627.7 4.7 exponential_select_fusion.2
  674.9 12.9 %fusion.79 = f32[3072,1024]{1,0:T(8,128)} fusion(bf16[1024,1024]{0,1:T(8,128)(2,1)} %bitcast.21, bf16[1024,1024]{0,1:T(8,128)(2,1)} %bitcast.153, bf16[1024,1024]{0,1:T(8,128)(2,1)S(1)} %bitcast.151, bf16[1024,1024]{0,1:T(8,128)(2,1)S(1)} %copy-done.4, f32[1024]{0:T(1024)S(1)} %copy-done.25, f32[1024]{0:T(1024)S(1)} %copy-done.23, f32[1024]{0:T(1024)S(1)} %copy-done.20), kind=kOutput, calls=%fused_computation.110 | convolution fusion | flops 6466568192 | bytes 20983808 | tf_op jit(solution)/shard_map/dot_general | solution.py:22
  687.9 13.1 %fusion.71 = (f32[1024]{0:T(1024)S(1)}, f32[1024]{0:T(1024)S(1)}, f32[1024]{0:T(1024)S(1)}, f32[1024,1024]{0,1:T(8,128)}) fusion(bf16[1024,1024]{0,1:T(8,128)(2,1)S(1)} %copy-done.4, f32[1024]{0:T(1024)S(1)} %copy-done.23, f32[1024]{0:T(1024)S(1)} %copy-done.20, f32[1024]{0:T(1024)S(1)} %copy-done.25, bf16[3072,1024]{1,0:T(8,128)(2,1)} %all-gather.6.cloned.1.call-done, ...), kind=kOutput, calls=%fused_computation.88 | convolution fusion | flops 6470759424 | bytes 18898944 | tf_op jit(solution)/shard_map/dot_general | solution.py:199
  701.0 39.9 %all-reduce.6 = (f32[1024]{0:T(1024)S(1)}, f32[1024]{0:T(1024)S(1)}) all-reduce(f32[1024]{0:T(1024)S(1)} %get-tuple-element.244, f32[1024]{0:T(1024)S(1)} %get-tuple-element.242), channel_id=6, replica_groups=mesh['fsdp'=32] {'fsdp'}, use_global_device_ids=true, to_apply=%region_22.23.clone | all-reduce | flops 2048 | bytes 16384
  742.0 28.5 %fusion.58 = f32[5248,1024]{1,0:T(8,128)} fusion(bf16[1024,2624]{1,0:T(8,128)(2,1)} %get-tuple-element.295, bf16[1024,2624]{1,0:T(8,128)(2,1)} %get-tuple-element.294, f32[1024,1024]{0,1:T(8,128)} %copy-done.7, f32[1024]{0:T(1024)S(1)} %convert_element_type.83, f32[1024]{0:T(1024)S(1)} %add_rsqrt_fusion, f32[1024]{0:T(1024)S(1)} %broadcast_multiply_fusion.6), kind=kOutput, calls=%fused_computation.70 | convolution fusion | flops 11031543808 | bytes 36450304 | tf_op jit(solution)/shard_map/dot_general | solution.py:22
  770.5 249.3 %fusion.4 = f32[168,1024]{1,0:T(8,128)S(1)} fusion(f32[5248,1024]{1,0:T(8,128)} %fusion.58), kind=kCustom, calls=%all-reduce-scatter | all-reduce-scatter fusion | flops 5505025 | bytes 22183936
  1020.6 9.9 collective-permute-start
  1030.5 11.7 %add_convert_fusion = bf16[1024,1024]{0,1:T(8,128)(2,1)} fusion(f32[1024,1024]{0,1:T(8,128)} %copy-done.7, bf16[1024,2624]{1,0:T(8,128)(2,1)} %get-tuple-element.296, bf16[1024,2624]{1,0:T(8,128)(2,1)} %all-gather.10.cloned.1.call-done), kind=kOutput, calls=%fused_computation.104 | convolution fusion | flops 5505024000 | bytes 17039360 | tf_op jit(solution)/shard_map/dot_general | solution.py:16
  1045.5 5.5 copy.70
  (379 shorter events, 408.2 us)
Async XLA Ops:
  7.2 76.2 %all-gather.6.cloned.1.call-start = ((), (), s32[]{:S(2)}) async-start(), calls=%async_computation.3 | async-start | bytes 6488064 | tf_op jit(solution)/shard_map/all_gather | solution.py:207
  7.9 215.7 %all-gather.8.cloned.1.call-start = ((), (), s32[]{:S(2)}) async-start(), calls=%async_computation.4 | async-start | bytes 2162688 | tf_op jit(solution)/shard_map/all_gather | solution.py:208
  8.6 223.2 %all-gather.12.cloned.1.call-start = ((), (), s32[]{:S(2)}) async-start(), calls=%async_computation.8 | async-start | bytes 11354112 | tf_op jit(solution)/shard_map/all_gather | solution.py:209
  9.4 289.7 %all-gather.10.cloned.1.call-start = ((), (), s32[]{:S(2)}) async-start(), calls=%async_computation.5 | async-start | bytes 5677056 | tf_op jit(solution)/shard_map/all_gather | solution.py:210
  10.0 1045.2 %reduce-scatter.10.cloned.1.call-start = ((), (), s32[]{:S(2)}) async-start(), calls=%async_computation.7 | async-start | bytes 4325376 | tf_op jit(solution)/shard_map/reduce_scatter | solution.py:233
  14.5 209.2 %copy-start.3 = (bf16[1024,1024]{0,1:T(8,128)(2,1)}, bf16[1024,1024]{0,1:T(8,128)(2,1)S(1)}, u32[]{:S(2)}) copy-start(bf16[1024,1024]{0,1:T(8,128)(2,1)S(1)} %copy.53) | copy-start | bytes 6291460
  14.8 77.8 %copy-start.19 = (f32[1024]{0:T(1024)}, f32[1024]{0:T(1024)S(1)}, u32[]{:S(2)}) copy-start(f32[1024]{0:T(1024)S(1)} %broadcast_multiply_fusion.7) | copy-start | bytes 12292
  15.5 77.2 %copy-start.22 = (f32[1024]{0:T(1024)}, f32[1024]{0:T(1024)S(1)}, u32[]{:S(2)}) copy-start(f32[1024]{0:T(1024)S(1)} %add_rsqrt_fusion.1) | copy-start | bytes 12292
  58.3 34.3 %copy-start.24 = (f32[1024]{0:T(1024)}, f32[1024]{0:T(1024)S(1)}, u32[]{:S(2)}) copy-start(f32[1024]{0:T(1024)S(1)} %convert_element_type.76) | copy-start | bytes 12292
  63.7 50.2 %copy-start.12 = (f32[1024,64]{0,1:T(8,128)}, f32[1024,64]{0,1:T(8,128)S(1)}, u32[]{:S(2)}) copy-start(f32[1024,64]{0,1:T(8,128)S(1)} %get-tuple-element.320) | copy-start | bytes 786436
  63.8 50.2 %copy-start.14 = (f32[1024,64]{0,1:T(8,128)}, f32[1024,64]{0,1:T(8,128)S(1)}, u32[]{:S(2)}) copy-start(f32[1024,64]{0,1:T(8,128)S(1)} %get-tuple-element.319) | copy-start | bytes 786436
  109.3 5.9 copy-start.2
  132.6 4.8 copy-start.21
  299.1 20.6 %copy-start.8 = (f32[1024,1024]{0,1:T(8,128)S(1)}, f32[1024,1024]{0,1:T(8,128)}, u32[]{:S(2)}) copy-start(f32[1024,1024]{0,1:T(8,128)} %copy-done.7) | copy-start | bytes 12582916
  346.0 6.4 copy-start.18
  356.9 698.2 %reduce-scatter.12.cloned.1.call-start = ((), (), s32[]{:S(2)}) async-start(), calls=%async_computation.9 | async-start | bytes 11354112
  388.6 666.5 %reduce-scatter.8.cloned.1.call-start = ((), (), s32[]{:S(2)}) async-start(), calls=%async_computation.6 | async-start | bytes 12976128 | tf_op jit(solution)/shard_map/reduce_scatter | solution.py:232
  389.1 272.6 %copy-start.13 = (f32[1024,64]{0,1:T(8,128)S(1)}, f32[1024,64]{0,1:T(8,128)}, u32[]{:S(2)}) copy-start(f32[1024,64]{0,1:T(8,128)} %copy-done.12) | copy-start | bytes 786436
  399.2 4.8 copy-start
  416.1 4.8 copy-start
  433.1 4.8 copy-start
  500.8 4.8 copy-start
  518.1 4.8 copy-start
  535.3 4.8 copy-start
  586.3 4.8 copy-start
  603.8 4.8 copy-start
  620.8 4.8 copy-start
  654.7 4.8 copy-start
  1020.6 32.9 %collective-permute-start = (f32[124,1024]{1,0:T(8,128)}, f32[124,1024]{1,0:T(8,128)S(1)}, u32[]{:S(2)}, u32[]{:S(2)}) collective-permute-start(f32[124,1024]{1,0:T(8,128)} %slice.84), channel_id=1, source_target_pairs={{0,1},{1,2},{2,3},{3,4},{4,5},{5,6},{6,7},{7,8},{8,9},{9,10},{10,1... | collective-permute-start | bytes 1523720
  1030.5 11.8 %copy-start.6 = (f32[1024,1024]{0,1:T(8,128)S(1)}, f32[1024,1024]{0,1:T(8,128)}, u32[]{:S(2)}) copy-start(f32[1024,1024]{0,1:T(8,128)} %copy-done.5) | copy-start | bytes 12582916
  1030.5 11.7 %copy-start.11 = (f32[1024,1024]{0,1:T(8,128)S(1)}, f32[1024,1024]{0,1:T(8,128)}, u32[]{:S(2)}) copy-start(f32[1024,1024]{0,1:T(8,128)} %get-tuple-element.318) | copy-start | bytes 12582916
  1045.5 5.5 copy-start.16
  (19 other events, 72.8 us)
Sparse Core Ops, SparseCore 0:
  10.9 72.4 all-gather.5
  86.2 54.8 all-gather.7
  144.0 87.7 all-gather.11
  234.6 64.4 all-gather.9
  357.0 139.9 reduce-scatter.9
  503.4 139.4 reduce-scatter.11
  688.0 193.7 reduce-scatter.7
where the time goes:
time: 1070 us; the launch traced here: 1060 us
  matrix products  479 us (45%)
  blocking collectives  332 us (31%)
  local copies, waits for them, and re-layouts  111 us (10%)
  other arithmetic  58.2 us (5%)
  waiting for transfers between devices  55.7 us (5%)
  between operations  14.8 us (1%)
    unnamed x3, blocking collectives  332 us
    dot_general x52, matrix products, matmul_nt(): lax.dot_general(left, right, (((1,), (1,)), ((), ())), preferred_element_...  207 us
    dot_general x36, matrix products, matmul_tn(): lax.dot_general(left, right, (((0,), (0,)), ((), ())), preferred_element_...  129 us
    unnamed x72, local copies, waits for them, and re-layouts  68.6 us
    dot_general x16, matrix products, per_head(): jnp.dot(grad_scores, key_head, preferred_element_type=jnp.float32) * scale  38.8 us
    dot_general x16, matrix products, per_head(): result = jnp.dot(weights, value_head, preferred_element_type=jnp.float32)  38.6 us
    all_gather x1, waiting for transfers between devices, body(): lax.all_gather(w_ff_out, 'fsdp', axis=0, tiled=True)  32.5 us
    dot_general x1, matrix products, ffn_backward(): jnp.dot(grad_inner, w_in, preferred_element_type=jnp.float32)  26.3 us
  transfers between devices with their start and end apart: 8, of which 3 were waited for; matrix products, arithmetic and copies ran while one was open for 78% of the time, Pallas kernels for 0%

commit v1 on v0

v1 whole, which is shorter than its diff:
```python
import functools
import math

import jax
import jax.numpy as jnp
from jax import lax
from jax.experimental import pallas as pl
from jax.experimental.pallas import tpu as pltpu
from jax.sharding import PartitionSpec as P

HD = 64
EPS = 1e-05
THETA = 160000.0
NEG = -1e30
LANES = 128
F32 = jnp.float32
BF16 = jnp.bfloat16
VMEM_BYTES = 60 << 20


def dot_nt(left, right):
    return lax.dot_general(left, right, (((1,), (1,)), ((), ())), preferred_element_type=F32)


def dot_nn(left, right):
    return lax.dot_general(left, right, (((1,), (0,)), ((), ())), preferred_element_type=F32)


def dot_tn(left, right):
    return lax.dot_general(left, right, (((0,), (0,)), ((), ())), preferred_element_type=F32)


def call(kernel, *, name, grid, in_specs, out_specs, out_shape, scratch=(), flops=0, nbytes=0, aliases=None):
    return pl.pallas_call(
        kernel,
        name=name,
        grid=grid,
        in_specs=in_specs,
        out_specs=out_specs,
        out_shape=out_shape,
        scratch_shapes=list(scratch),
        input_output_aliases=aliases or {},
        compiler_params=pltpu.CompilerParams(
            dimension_semantics=("arbitrary",) * len(grid), vmem_limit_bytes=VMEM_BYTES
        ),
        cost_estimate=pl.CostEstimate(flops=flops, transcendentals=0, bytes_accessed=nbytes),
    )


def sds(shape, dtype):
    return jax.ShapeDtypeStruct(shape, dtype)


def whole(shape):
    zeros = (0,) * len(shape)
    return pl.BlockSpec(shape, lambda *_: zeros)


def normalise(field):
    centre = jnp.mean(field, axis=-1, keepdims=True)
    centered = field - centre
    variance = jnp.mean(centered * centered, axis=-1, keepdims=True)
    inverse = lax.rsqrt(variance + EPS)
    return centered * inverse, inverse


def minus_row(field, row):
    return (field.reshape(-1, *row.shape) - row[None]).reshape(field.shape)


def swap_halves(field):
    lane = lax.broadcasted_iota(jnp.int32, field.shape, 1)
    first = (lane & (HD - 1)) < HD // 2
    return jnp.where(
        first, pltpu.roll(field, LANES - HD // 2, 1), pltpu.roll(field, HD // 2, 1)
    )


def fetch(weights, at, rows, target, sem):
    order_ref, pieces = weights
    i = 0
    for piece in pieces:
        for slot in range(piece.shape[0]):
            start = pl.multiple_of(order_ref[i] * rows, rows)
            pltpu.make_async_copy(
                piece.at[slot, pl.ds(at, rows), :], target.at[pl.ds(start, rows), :], sem
            ).start()
            i += 1


def arrive(target, sem):
    pltpu.make_async_copy(target, target, sem).wait()


def fetching_call(
    kernel, weights, *, name, grid, in_specs, out_specs, out_shape, scratch=(), flops=0, nbytes=0
):
    number = len(weights)

    def run(*refs):
        orders, rest, sets = refs[:number], refs[number:], []
        for order, (_, pieces) in zip(orders, weights, strict=True):
            sets.append((order, rest[: len(pieces)]))
            rest = rest[len(pieces) :]
        kernel(*sets, *rest)

    pieces = [piece for _, some in weights for piece in some]
    made = pl.pallas_call(
        run,
        name=name,
        grid_spec=pltpu.PrefetchScalarGridSpec(
            num_scalar_prefetch=number,
            grid=grid,
            in_specs=[pl.BlockSpec(memory_space=pl.ANY)] * len(pieces) + in_specs,
            out_specs=out_specs,
            scratch_shapes=list(scratch),
        ),
        out_shape=out_shape,
        compiler_params=pltpu.CompilerParams(
            dimension_semantics=("arbitrary",) * len(grid), vmem_limit_bytes=VMEM_BYTES
        ),
        cost_estimate=pl.CostEstimate(flops=flops, transcendentals=0, bytes_accessed=nbytes),
    )
    return lambda *args: made(*[order for order, _ in weights], *pieces, *args)


def project_kernel(
    rope_blocks, query_blocks, rows, weights,
    tok_ref, gain_ref, cos_ref, sin_ref, out_ref, hid_ref, w_ref, sem,
):
    step = pl.program_id(0)
    block = out_ref.shape[1]

    @pl.when(step == 0)
    def _():
        fetch(weights, 0, rows, w_ref, sem)
        normed, _ = normalise(tok_ref[...].astype(F32))
        hid_ref[...] = (normed * gain_ref[...]).astype(BF16)
        arrive(w_ref, sem)

    acc = dot_nt(hid_ref[...], w_ref[pl.ds(pl.multiple_of(step * block, block), block), :])

    @pl.when(step < rope_blocks)
    def _():
        scale = jnp.where(step < query_blocks, 1.0 / math.sqrt(HD), 1.0).astype(F32)
        cosine, sine = cos_ref[...], sin_ref[...]
        for s in range(acc.shape[1] // LANES):
            part = acc[:, s * LANES : (s + 1) * LANES]
            turned = part * cosine + swap_halves(part) * sine
            out_ref[:, s * LANES : (s + 1) * LANES] = (turned * scale).astype(BF16)

    @pl.when(step >= rope_blocks)
    def _():
        out_ref[...] = acc.astype(BF16)


def project(tokens, gain, cosine, sine, weights, rows):
    count, width = tokens.shape
    total = 3 * width
    block = 512
    return fetching_call(
        functools.partial(project_kernel, 2 * width // block, width // block, rows),
        [weights],
        name="norm_project",
        grid=(total // block,),
        in_specs=[
            whole((count, width)),
            whole((1, width)),
            whole((count, LANES)),
            whole((count, LANES)),
        ],
        out_specs=[pl.BlockSpec((count, block), lambda j, *_: (0, j)), whole((count, width))],
        out_shape=[sds((count, total), BF16), sds((count, width), BF16)],
        scratch=[pltpu.VMEM((total, width), BF16), pltpu.SemaphoreType.DMA],
        flops=2 * count * width * total,
        nbytes=2 * (2 * count * width + total * width + total * count),
    )(tokens, gain, cosine, sine)


def attend_kernel(chunk, q_ref, k_ref, v_ref, segc_ref, segr_ref, out_ref, lse_ref, vt_ref, ot_ref):
    count = q_ref.shape[0]
    vt_ref[...] = v_ref[...].T
    keys = k_ref[...]
    lane = lax.broadcasted_iota(jnp.int32, (chunk, LANES), 1)

    def body(c, _):
        at = pl.ds(pl.multiple_of(c * chunk, chunk), chunk)
        query = q_ref[at, :]
        column = segc_ref[...]
        allowed = jnp.concatenate([column] * (chunk // LANES), axis=1) == segr_ref[:, at]
        for h in range(2):
            picked = jnp.where((lane >= h * HD) & (lane < (h + 1) * HD), query, jnp.zeros_like(query))
            scores = jnp.where(allowed, dot_nt(keys, picked), NEG)
            top = jnp.max(scores, axis=0, keepdims=True)
            powers = jnp.exp(scores - top)
            total = jnp.sum(powers, axis=0, keepdims=True)
            lse_ref[0, pl.ds(h, 1), at] = top + jnp.log(total)
            mixed = dot_nn(vt_ref[h * HD : (h + 1) * HD, :], powers.astype(BF16))
            ot_ref[h * HD : (h + 1) * HD, at] = mixed / total
        return 0

    lax.fori_loop(0, count // chunk, body, 0)
    out_ref[...] = ot_ref[...].T.astype(BF16)


def attend(qkv, seg_column, seg_row, width, first, number, before=None):
    count = qkv.shape[0]
    pairs = width // LANES
    chunk = 256
    kept = () if before is None else tuple(before)

    def kernel(*refs):
        attend_kernel(chunk, *refs[:5], *refs[5 + len(kept) :])

    tall = lambda offset: pl.BlockSpec((count, LANES), lambda p: (0, offset + first + p))
    return call(
        kernel,
        name="attend",
        grid=(number,),
        in_specs=[tall(0), tall(pairs), tall(2 * pairs), whole((count, LANES)), whole((1, count))]
        + [pl.BlockSpec(memory_space=pl.ANY)] * len(kept),
        out_specs=[tall(0), pl.BlockSpec((1, 2, count), lambda p: (first + p, 0, 0))],
        out_shape=[sds((count, width), BF16), sds((pairs, 2, count), F32)],
        scratch=[pltpu.VMEM((LANES, count), BF16), pltpu.VMEM((LANES, count), F32)],
        flops=16 * count * count * LANES * number,
        nbytes=2 * 4 * count * LANES * number,
        aliases={5: 0, 6: 1} if kept else None,
    )(qkv, qkv, qkv, seg_column, seg_row, *kept)


def attend_back_kernel(
    chunk, q_ref, k_ref, v_ref, o_ref, g_ref, lse_ref, segc_ref, segr_ref, cos_ref, sin_ref,
    out_ref, kt_ref, dk_ref, dv_ref, dqt_ref, delta_ref, total_ref,
):
    count = q_ref.shape[0]
    kt_ref[...] = k_ref[...].T
    keys, values = k_ref[...], v_ref[...]
    product = (g_ref[...].astype(F32) * o_ref[...].astype(F32)).T
    for h in range(2):
        row = jnp.sum(product[h * HD : (h + 1) * HD, :], axis=0, keepdims=True)
        delta_ref[h] = jnp.broadcast_to(row, (8, count))
        total_ref[h] = jnp.broadcast_to(lse_ref[0, h : h + 1, :], (8, count))
    dk_ref[...] = jnp.zeros_like(dk_ref)
    dv_ref[...] = jnp.zeros_like(dv_ref)
    lane = lax.broadcasted_iota(jnp.int32, (chunk, LANES), 1)

    def body(c, _):
        at = pl.ds(pl.multiple_of(c * chunk, chunk), chunk)
        query, grad = q_ref[at, :], g_ref[at, :]
        column = segc_ref[...]
        allowed = jnp.concatenate([column] * (chunk // LANES), axis=1) == segr_ref[:, at]
        turned = []
        for h in range(2):
            mine = (lane >= h * HD) & (lane < (h + 1) * HD)
            query_h = jnp.where(mine, query, jnp.zeros_like(query))
            grad_h = jnp.where(mine, grad, jnp.zeros_like(grad))
            scores = jnp.where(allowed, dot_nt(keys, query_h), NEG)
            weights = jnp.exp(minus_row(scores, total_ref[h, :, at]))
            dv_ref[...] += dot_nn(weights.astype(BF16), grad_h)
            spread = minus_row(dot_nt(values, grad_h), delta_ref[h, :, at])
            grad_scores = (weights * spread).astype(BF16)
            dk_ref[...] += dot_nn(grad_scores, query_h)
            turned.append(dot_nn(kt_ref[...], grad_scores))
        row = lax.broadcasted_iota(jnp.int32, (LANES, chunk), 0)
        dqt_ref[:, at] = jnp.where(row < HD, turned[0], turned[1])
        return 0

    lax.fori_loop(0, count // chunk, body, 0)
    cosine, sine = cos_ref[...], sin_ref[...]
    grad_query = dqt_ref[...].T * (1.0 / math.sqrt(HD))
    out_ref[0] = (grad_query * cosine - swap_halves(grad_query) * sine).astype(BF16)
    grad_key = dk_ref[...]
    out_ref[1] = (grad_key * cosine - swap_halves(grad_key) * sine).astype(BF16)
    out_ref[2] = dv_ref[...].astype(BF16)


def attend_back(qkv, attn_out, grad_heads, lse, seg_column, seg_row, cosine, sine, first, number, before=None):
    count, width = attn_out.shape
    pairs = width // LANES
    chunk = 256
    kept = () if before is None else (before,)

    def kernel(*refs):
        attend_back_kernel(chunk, *refs[:10], *refs[10 + len(kept) :])

    tall = lambda offset: pl.BlockSpec((count, LANES), lambda p: (0, offset + first + p))
    return call(
        kernel,
        name="attend_back",
        grid=(number,),
        in_specs=[
            tall(0),
            tall(pairs),
            tall(2 * pairs),
            tall(0),
            tall(0),
            pl.BlockSpec((1, 2, count), lambda p: (first + p, 0, 0)),
            whole((count, LANES)),
            whole((1, count)),
            whole((count, LANES)),
            whole((count, LANES)),
        ]
        + [pl.BlockSpec(memory_space=pl.ANY)] * len(kept),
        out_specs=pl.BlockSpec((3, count, LANES), lambda p: (0, 0, first + p)),
        out_shape=sds((3, count, width), BF16),
        scratch=[
            pltpu.VMEM((LANES, count), BF16),
            pltpu.VMEM((count, LANES), F32),
            pltpu.VMEM((count, LANES), F32),
            pltpu.VMEM((LANES, count), F32),
            pltpu.VMEM((2, 8, count), F32),
            pltpu.VMEM((2, 8, count), F32),
        ],
        flops=40 * count * count * LANES * number,
        nbytes=2 * 8 * count * LANES * number,
        aliases={10: 0} if kept else None,
    )(qkv, qkv, qkv, attn_out, grad_heads, lse, seg_column, seg_row, cosine, sine, *kept)


def join_kernel(rows, weights, tok_ref, attn_ref, gain_ref, resid_ref, hid_ref, w_ref, sem):
    @pl.when(pl.program_id(0) == 0)
    def _():
        fetch(weights, 0, rows, w_ref, sem)
        arrive(w_ref, sem)

    resid = tok_ref[...].astype(F32) + dot_nt(attn_ref[...], w_ref[...])
    resid_ref[...] = resid
    normed, _ = normalise(resid)
    hid_ref[...] = (normed * gain_ref[...]).astype(BF16)


def join(tokens, attn_out, gain, weights, rows_out):
    count, width = tokens.shape
    block = 256
    rows = pl.BlockSpec((block, width), lambda i, *_: (i, 0))
    return fetching_call(
        functools.partial(join_kernel, rows_out),
        [weights],
        name="attn_out_norm",
        grid=(count // block,),
        in_specs=[rows, rows, whole((1, width))],
        out_specs=[rows, rows],
        out_shape=[sds((count, width), F32), sds((count, width), BF16)],
        scratch=[pltpu.VMEM((width, width), BF16), pltpu.SemaphoreType.DMA],
        flops=2 * count * width * width,
        nbytes=2 * 6 * count * width,
    )(tokens, attn_out, gain)


def ffn_kernel(
    rows_in, at, rows_ff, weights_in, weights_rest,
    resid_ref, hid_ref, cot_ref, gain_ref,
    out_ref, mid_ref, low_ref, gnorm_ref, g_in_ref, g_out_ref,
    cot_t_ref, out_acc, hid_acc, w_in_ref, w_ff_ref, sem_in, sem_ff,
):
    step = pl.program_id(0)
    block = g_out_ref.shape[1]
    units = w_in_ref.shape[0] // 2
    width = hid_ref.shape[1]

    @pl.when(step == 0)
    def _():
        fetch(weights_in, 0, rows_in, w_in_ref, sem_in)
        for b in range(w_ff_ref.shape[0]):
            fetch(weights_rest, at + b * rows_ff, rows_ff, w_ff_ref.at[b], sem_ff)
        cot_t_ref[...] = cot_ref[...].T
        out_acc[...] = jnp.zeros_like(out_acc)
        hid_acc[...] = jnp.zeros_like(hid_acc)
        arrive(w_in_ref, sem_in)
        arrive(w_ff_ref, sem_ff)

    hidden = hid_ref[...]
    w_pre = w_in_ref[pl.ds(pl.multiple_of(step * block, block), block), :]
    w_gate = w_in_ref[pl.ds(pl.multiple_of(units + step * block, block), block), :]
    per = width // block
    w_out = w_ff_ref[step // per, :, pl.ds(pl.multiple_of(step % per * block, block), block)]
    pre = dot_nt(hidden, w_pre)
    gate = dot_nt(hidden, w_gate)
    grad_mixed = dot_nn(cot_ref[...], w_out)
    cdf = 0.5 * (1.0 + lax.erf(pre * 0.7071067811865476))
    density = jnp.exp(-0.5 * pre * pre) * 0.3989422804014327
    gelu = pre * cdf
    mixed = (gelu * gate).astype(BF16)
    out_acc[...] += dot_nt(mixed, w_out)
    g_out_ref[...] = dot_nn(cot_t_ref[...], mixed).astype(BF16)
    grad_pre = (grad_mixed * gate * (cdf + pre * density)).astype(BF16)
    grad_gate = (grad_mixed * gelu).astype(BF16)
    g_in_ref[0] = dot_tn(grad_pre, hidden).astype(BF16)
    g_in_ref[1] = dot_tn(grad_gate, hidden).astype(BF16)
    hid_acc[...] += dot_nn(grad_pre, w_pre) + dot_nn(grad_gate, w_gate)

    @pl.when(step == pl.num_programs(0) - 1)
    def _():
        rows = 256
        gnorm = jnp.zeros_like(gnorm_ref)
        for i in range(resid_ref.shape[0] // rows):
            at = slice(i * rows, (i + 1) * rows)
            resid = resid_ref[at, :]
            out_ref[at, :] = (resid + out_acc[at, :]).astype(BF16)
            normed, inverse = normalise(resid)
            grad = hid_acc[at, :]
            gnorm += jnp.sum(grad * normed, axis=0, keepdims=True)
            hat = grad * gain_ref[...]
            first = jnp.mean(hat, axis=-1, keepdims=True)
            second = jnp.mean(hat * normed, axis=-1, keepdims=True)
            mid = cot_ref[at, :].astype(F32) + inverse * (hat - first - normed * second)
            mid_ref[at, :] = mid
            low_ref[at, :] = mid.astype(BF16)
        gnorm_ref[...] = gnorm


def ffn(resid, hidden, cotangent, gain, w_in, w_rest, units, rows_in, at, rows_ff):
    count, width = resid.shape
    block = 256
    spans = -(-units // width)
    once = pl.BlockSpec((count, width), lambda *_: (0, 0), pipeline_mode=pl.Buffered(1))
    return fetching_call(
        functools.partial(ffn_kernel, rows_in, at, rows_ff),
        [w_in, w_rest],
        name="ffn_forward_backward",
        grid=(units // block,),
        in_specs=[once, once, once, whole((1, width))],
        out_specs=[
            once,
            once,
            once,
            whole((1, width)),
            pl.BlockSpec((2, block, width), lambda j, *_: (0, j, 0)),
            pl.BlockSpec((width, block), lambda j, *_: (0, j)),
        ],
        out_shape=[
            sds((count, width), BF16),
            sds((count, width), F32),
            sds((count, width), BF16),
            sds((1, width), F32),
            sds((2, units, width), BF16),
            sds((width, units), BF16),
        ],
        scratch=[
            pltpu.VMEM((width, count), BF16),
            pltpu.VMEM((count, width), F32),
            pltpu.VMEM((count, width), F32),
            pltpu.VMEM((2 * units, width), BF16),
            pltpu.VMEM((spans, width, width), BF16),
            pltpu.SemaphoreType.DMA,
            pltpu.SemaphoreType.DMA,
        ],
        flops=18 * count * width * units,
        nbytes=2 * (10 * count * width + 6 * units * width),
    )(resid, hidden, cotangent, gain)


def join_back_kernel(rows, weights, low_ref, attn_ref, heads_ref, gw_ref, w_ref, sem):
    step = pl.program_id(0)
    block = heads_ref.shape[1]

    @pl.when(step == 0)
    def _():
        fetch(weights, 0, rows, w_ref, sem)
        arrive(w_ref, sem)

    span = pl.ds(pl.multiple_of(step * block, block), block)
    heads_ref[...] = dot_nn(low_ref[...], w_ref[:, span]).astype(BF16)
    gw_ref[...] = dot_tn(low_ref[:, span], attn_ref[...]).astype(BF16)


def join_back(low, attn_out, weights, rows):
    count, width = low.shape
    block = 256
    return fetching_call(
        functools.partial(join_back_kernel, rows),
        [weights],
        name="attn_out_back",
        grid=(width // block,),
        in_specs=[whole((count, width)), whole((count, width))],
        out_specs=[pl.BlockSpec((count, block), lambda j, *_: (0, j)), pl.BlockSpec((block, width), lambda j, *_: (j, 0))],
        out_shape=[sds((count, width), BF16), sds((width, width), BF16)],
        scratch=[pltpu.VMEM((width, width), BF16), pltpu.SemaphoreType.DMA],
        flops=4 * count * width * width,
        nbytes=2 * 5 * count * width,
    )(low, attn_out)


def project_grad_kernel(gp_ref, hid_ref, out_ref):
    out_ref[...] = dot_tn(gp_ref[0], hid_ref[...]).astype(BF16)


def project_grad(grad_projected, hidden):
    count, width = hidden.shape
    block = 512
    per = width // block
    return call(
        project_grad_kernel,
        name="grad_qkv",
        grid=(3 * per,),
        in_specs=[pl.BlockSpec((1, count, block), lambda j: (j // per, 0, j % per)), whole((count, width))],
        out_specs=pl.BlockSpec((block, width), lambda j: (j, 0)),
        out_shape=sds((3 * width, width), BF16),
        flops=6 * count * width * width,
        nbytes=2 * 7 * count * width,
    )(grad_projected, hidden)


def project_back_kernel(
    rows_qkv, weights, gp_ref, tok_ref, mid_ref, gain_ref, out_ref, gnorm_ref, acc_ref, w_ref, sem
):
    step = pl.program_id(0)
    width = gp_ref.shape[2]

    @pl.when(step == 0)
    def _():
        fetch(weights, 0, rows_qkv, w_ref, sem)
        arrive(w_ref, sem)

    term = dot_nn(gp_ref[0], w_ref[pl.ds(pl.multiple_of(step * width, width), width), :])

    @pl.when(step == 0)
    def _():
        acc_ref[...] = term

    @pl.when(step > 0)
    def _():
        acc_ref[...] += term

    @pl.when(step == pl.num_programs(0) - 1)
    def _():
        rows = 256
        gnorm = jnp.zeros_like(gnorm_ref)
        for i in range(tok_ref.shape[0] // rows):
            at = slice(i * rows, (i + 1) * rows)
            normed, inverse = normalise(tok_ref[at, :].astype(F32))
            grad = acc_ref[at, :]
            gnorm += jnp.sum(grad * normed, axis=0, keepdims=True)
            hat = grad * gain_ref[...]
            first = jnp.mean(hat, axis=-1, keepdims=True)
            second = jnp.mean(hat * normed, axis=-1, keepdims=True)
            out_ref[at, :] = mid_ref[at, :] + inverse * (hat - first - normed * second)
        gnorm_ref[...] = gnorm


def project_back(grad_projected, weights, rows_qkv, tokens, mid, gain):
    count, width = tokens.shape
    full = whole((count, width))
    return fetching_call(
        functools.partial(project_back_kernel, rows_qkv),
        [weights],
        name="grad_tokens",
        grid=(3,),
        in_specs=[
            pl.BlockSpec((1, count, width), lambda j, *_: (j, 0, 0)),
            full,
            full,
            whole((1, width)),
        ],
        out_specs=[full, whole((1, width))],
        out_shape=[sds((count, width), F32), sds((1, width), F32)],
        scratch=[
            pltpu.VMEM((count, width), F32),
            pltpu.VMEM((3 * width, width), BF16),
            pltpu.SemaphoreType.DMA,
        ],
        flops=6 * count * width * width,
        nbytes=2 * 12 * count * width,
    )(grad_projected, tokens, mid, gain)


Z, Y, X = 4, 2, 2
UP, DOWN, IN_Y, IN_X = (1, 0, 0), (-1, 0, 0), (0, 1, 0), (0, 0, 1)
CROSSED, LEVEL = ("planes", "lines"), ("planes", "planes")
SPREAD = {
    CROSSED: (((UP, IN_X), (DOWN, IN_Y), (UP, IN_Y)), ((IN_Y, UP), (IN_X, DOWN), (IN_X, UP))),
    LEVEL: (((UP, UP), (DOWN, DOWN), (UP, UP)), ((IN_Y, IN_X), (IN_X, IN_Y), (IN_X, IN_Y))),
}
REDUCE = {
    CROSSED: (((IN_X, DOWN), (IN_X, UP), (IN_Y, DOWN)), ((DOWN, IN_Y), (UP, IN_Y), (DOWN, IN_X))),
    LEVEL: (((IN_X, IN_Y), (IN_X, IN_Y), (IN_Y, IN_X)), ((DOWN, DOWN), (UP, UP), (DOWN, DOWN))),
}


def ident(z, y, x, c):
    return (((z % Z) * Y + y % Y) * X + x % X) * 2 + c


def plus(*moves):
    return tuple(sum(m[i] for m in moves) for i in range(3))


def minus(move):
    return tuple(-m for m in move)


def hop(array, axis, moves):
    pairs = [
        (ident(z, y, x, c), ident(z + m[0], y + m[1], x + m[2], c))
        for z in range(Z) for y in range(Y) for x in range(X)
        for c, m in enumerate(moves)
    ]
    return lax.ppermute(array, axis, pairs)


def swap_cores(array, axis):
    return lax.ppermute(array, axis, [(i, i ^ 1) for i in range(2 * Z * Y * X)])


def place(axis):
    me = lax.axis_index(axis)
    return (me // (2 * Y * X), me // (2 * X) % Y, me // 2 % X), me % 2


def by_core(c, zero, one):
    return jnp.where(c == 0, jnp.stack(zero), jnp.stack(one)).astype(jnp.int32)


def tie(*values):
    return lax.optimization_barrier(values)


class Spread:
    def __init__(self, shard, axis, route):
        self.shard, self.axis, self.route = shard, axis, route

    def near(self):
        short, _ = SPREAD[self.route]
        self.first = hop(self.shard, self.axis, short[0])
        self.third = hop(self.shard, self.axis, short[1])

    def nearer(self):
        short, _ = SPREAD[self.route]
        second = hop(self.first, self.axis, short[2])
        self.block = jnp.stack([self.shard, self.first, second, self.third])

    def far(self):
        _, far = SPREAD[self.route]
        self.one = hop(self.block, self.axis, far[0])
        self.three = hop(self.block, self.axis, far[1])

    def farther(self):
        _, far = SPREAD[self.route]
        self.two = hop(self.one, self.axis, far[2])

    def result(self):
        short, far = SPREAD[self.route]
        mine = (self.block, self.one, self.two, self.three)
        pieces = mine + tuple(swap_cores(b, self.axis) for b in mine)
        at, c = place(self.axis)
        froms = []
        for core in range(2):
            s, f = [m[core] for m in short], [m[core] for m in far]
            close = [(0, 0, 0), s[0], plus(s[0], s[2]), s[1]]
            long = [(0, 0, 0), f[0], plus(f[0], f[2]), f[1]]
            froms.append([ident(*plus(at, minus(a), minus(b)), core) for a in long for b in close])
        order = jnp.concatenate([by_core(c, *froms), by_core(c, *froms[::-1])])
        return order, pieces


def lay_out(grad, wide):
    spans = [(b, min(b + wide, grad.shape[2])) for b in range(0, grad.shape[2], wide)]
    return spans, grad.shape[1] * len(spans)


def collect(grads, twins, extras, chosen, lines, wide, dtype):
    four = chosen.shape[1]
    total = sum(lay_out(g, wide)[1] for g in grads)
    k, number = len(grads) * four, len(lines)

    def kernel(chosen_ref, *refs):
        mine, theirs, more, outs = refs[:k], refs[k : 2 * k], refs[2 * k : -number], refs[-number:]

        def fill(out):
            for i in range(four):
                at = 0
                for g, t in zip(mine[i::four], theirs[i::four], strict=True):
                    rows = g.shape[1]
                    for a, b in lay_out(g, wide)[0]:
                        value = g[0, :, a:b].astype(F32) + t[0, :, a:b].astype(F32)
                        for m in more:
                            value = value + m[i, at : at + rows, : b - a].astype(F32)
                        out[i, at : at + rows, : b - a] = value.astype(dtype)
                        if b - a < wide:
                            out[i, at : at + rows, b - a :] = jnp.zeros((rows, wide - (b - a)), dtype)
                        at += rows

        for j, out in enumerate(outs):
            pl.when(pl.program_id(0) == j)(functools.partial(fill, out))

    def by_device(g, i):
        def index(j, chosen_ref):
            device = chosen_ref[lines[0], i]
            for step, which in enumerate(lines[1:], 1):
                device = jnp.where(j == step, chosen_ref[which, i], device)
            return device, 0, 0

        return pl.BlockSpec((1, *g.shape[1:]), index)

    devices = [by_device(g, i) for g in grads for i in range(four)]
    every = [g for g in grads for _ in range(four)]
    pairs = [t for t in twins for _ in range(four)]
    block = whole((four, total, wide))
    return pl.pallas_call(
        kernel,
        name="collect_grads",
        grid_spec=pltpu.PrefetchScalarGridSpec(
            num_scalar_prefetch=1,
            grid=(number,),
            in_specs=devices * 2 + [block] * len(extras),
            out_specs=[block] * number,
        ),
        out_shape=[sds((four, total, wide), dtype)] * number,
        compiler_params=pltpu.CompilerParams(
            dimension_semantics=("arbitrary",), vmem_limit_bytes=VMEM_BYTES
        ),
        cost_estimate=pl.CostEstimate(
            flops=number * four * total * wide * (1 + len(extras)),
            transcendentals=0,
            bytes_accessed=2 * number * four * total * wide * (3 + len(extras)),
        ),
    )(chosen, *every, *pairs, *extras)


class Reduce:
    def __init__(self, axis, route, wide):
        self.axis, self.route, self.wide = axis, route, wide
        far, short = REDUCE[route]
        at, c = place(axis)
        both = lambda a, b: tuple(plus(i, j) for i, j in zip(a, b, strict=True))
        here = ((0, 0, 0), (0, 0, 0))

        def line(step):
            lists = []
            for core, kind in enumerate(route):
                z, y, x = plus(at, step[core])
                if kind == "planes":
                    lists.append([ident(k, y, x, core) for k in range(Z)])
                else:
                    lists.append([ident(z, j, k, core) for j in range(Y) for k in range(X)])
            return by_core(c, *lists)

        def slot(step):
            places = []
            for core, kind in enumerate(route):
                z, y, x = plus(at, step[core])
                places.append(z % Z if kind == "planes" else y % Y * X + x % X)
            return jnp.where(c == 0, places[0], places[1])

        self.chosen = jnp.stack([line(s) for s in (both(far[0], far[2]), far[1], far[2], here)])
        self.slots = [slot(s) for s in (both(short[0], short[2]), short[1], short[2], here)]

    def pair(self, grads):
        self.grads = grads
        self.twins = tuple(swap_cores(g, self.axis) for g in grads)

    def pack(self):
        self.one, self.two = collect(self.grads, self.twins, (), self.chosen, (0, 1), self.wide, BF16)

    def far(self):
        far, _ = REDUCE[self.route]
        self.one, self.two = hop(self.one, self.axis, far[0]), hop(self.two, self.axis, far[1])

    def repack(self):
        (self.three,) = collect(self.grads, self.twins, (self.one,), self.chosen, (2,), self.wide, BF16)

    def farther(self):
        far, _ = REDUCE[self.route]
        self.three = hop(self.three, self.axis, far[2])

    def pick(self, which):
        return lax.dynamic_index_in_dim(self.block, self.slots[which], 0, keepdims=False)

    def gather(self):
        (self.block,) = collect(self.grads, self.twins, (self.two, self.three), self.chosen, (3,), self.wide, F32)

    def near(self):
        _, short = REDUCE[self.route]
        self.one = hop(self.pick(0).astype(BF16), self.axis, short[0])
        self.two = hop(self.pick(1).astype(BF16), self.axis, short[1])

    def nearer(self):
        _, short = REDUCE[self.route]
        self.three = hop((self.pick(2) + self.one.astype(F32)).astype(BF16), self.axis, short[2])

    def result(self):
        return self.pick(3) + self.two.astype(F32) + self.three.astype(F32)


def gains_kernel(at, number, weights, out_ref, rows_ref, sem):
    fetch(weights, at, 8, rows_ref, sem)
    arrive(rows_ref, sem)
    total, width = rows_ref.shape
    devices = total // 8
    owner = lax.broadcasted_iota(jnp.int32, (devices, total), 0)
    row = lax.broadcasted_iota(jnp.int32, (devices, total), 1)
    found = dot_nn((row == owner * 8).astype(BF16), rows_ref[:, :LANES]).astype(BF16)
    place_in = lax.broadcasted_iota(jnp.int32, (LANES, width), 0)
    lane = lax.broadcasted_iota(jnp.int32, (LANES, width), 1)
    mine = lax.broadcasted_iota(jnp.int32, (devices, width), 1) // number
    mine = mine == lax.broadcasted_iota(jnp.int32, (devices, width), 0)
    for which in range(2):
        tiled = dot_nn(found, (place_in == lane % number + which * number).astype(BF16))
        out_ref[which : which + 1, :] = jnp.sum(jnp.where(mine, tiled, 0.0), axis=0, keepdims=True)


def find_gains(weights, at, width):
    devices = weights[0].shape[0]
    return fetching_call(
        functools.partial(gains_kernel, at, width // devices),
        [weights],
        name="norm_scales",
        grid=(1,),
        in_specs=[],
        out_specs=[whole((2, width))],
        out_shape=[sds((2, width), F32)],
        scratch=[pltpu.VMEM((devices * 8, width), BF16), pltpu.SemaphoreType.DMA],
        nbytes=2 * devices * 8 * width,
    )()[0]


def tables(segment):
    count = segment.shape[0]
    slots = jnp.arange(count, dtype=jnp.int32)
    order = jnp.where(segment < 0, count, segment)
    starts = jnp.sum((order[None, :] < order[:, None]).astype(jnp.int32), axis=1)
    positions = (slots - starts).astype(F32)
    half = HD // 2
    freqs = THETA ** (-2.0 * jnp.arange(half, dtype=F32) / HD)
    angles = positions[:, None] * freqs[None, :]
    cosine, sine = jnp.cos(angles), jnp.sin(angles)
    cosine = jnp.concatenate([cosine] * 4, axis=1)
    sine = jnp.concatenate([-sine, sine] * 2, axis=1)
    group = jnp.where(segment < 0, -1 - slots, segment)
    return cosine, sine, jnp.broadcast_to(group[:, None], (count, LANES)), group[None, :]


def spans_of(matrix, wide):
    rows, columns = matrix.shape
    count = -(-columns // wide)
    matrix = jnp.pad(matrix, ((0, 0), (0, count * wide - columns)))
    return matrix.reshape(rows, count, wide).transpose(1, 0, 2).reshape(count * rows, wide)


def finish(g_in, g_ff, rows_in, padded, n, axis, g_one, g_two):
    g_in = g_in[:rows_in]
    g_ff = g_ff.reshape(-1, n // 2, padded)[:, :, :rows_in].reshape(-1, n // 2 * rows_in)
    g_norms = jnp.stack([g_one.reshape(n, -1), g_two.reshape(n, -1)], axis=1)
    g_norms = jnp.sum(lax.all_to_all(g_norms, axis, 0, 0, tiled=True), axis=0)
    return g_in, g_ff, g_norms


def by_collectives(tokens, cotangent, segment, w_qkv, w_attn_out, w_in, w_ff_out, gains, padded, axis):
    n = lax.axis_size(axis)
    width = tokens.shape[1]
    units = n // 2 * padded
    pairs = width // LANES
    gather = lambda shard: lax.all_gather(shard, axis, axis=0, tiled=True)
    at_once = lambda matrix: (jnp.zeros((1,), jnp.int32), (matrix[None],))
    w_qkv, w_in = at_once(gather(w_qkv)), at_once(gather(w_in))
    w_rest = at_once(jnp.concatenate([gather(w_attn_out), spans_of(gather(w_ff_out), width)]))
    gains = gather(gains[None]).astype(F32)
    gain_one, gain_two = (g.reshape(1, width) for g in jnp.split(gains, 2, axis=1))
    cosine, sine, seg_column, seg_row = tables(segment)
    qkv, hidden_one = project(tokens, gain_one, cosine, sine, w_qkv, 3 * width)
    attn_out, lse = attend(qkv, seg_column, seg_row, width, 0, pairs)
    resid, hidden_two = join(tokens, attn_out, gain_two, w_rest, width)
    output, mid, low, g_two, g_in, g_ff = ffn(
        resid, hidden_two, cotangent, gain_two, w_in, w_rest, units, 2 * units, width, width
    )
    grad_heads, g_out = join_back(low, attn_out, w_rest, width)
    grad_projected = attend_back(qkv, attn_out, grad_heads, lse, seg_column, seg_row, cosine, sine, 0, pairs)
    g_qkv = project_grad(grad_projected, hidden_one)
    grad_tokens, g_one = project_back(grad_projected, w_qkv, 3 * width, tokens, mid, gain_one)
    scatter = lambda grad: lax.psum_scatter(grad, axis, scatter_dimension=0, tiled=True).astype(F32)
    g_in = g_in.reshape(2 * units, width)
    return output, grad_tokens, scatter(g_qkv), scatter(g_out), scatter(g_in), scatter(g_ff), g_one, g_two


def by_links(tokens, cotangent, segment, w_qkv, w_attn_out, w_in, w_ff_out, gains, padded, axis):
    n = lax.axis_size(axis)
    width = tokens.shape[1]
    units = n // 2 * padded
    pairs = width // LANES
    rows_qkv, rows_out, rows_ff = w_qkv.shape[0], w_attn_out.shape[0], w_ff_out.shape[0]
    gain_rows = jnp.pad(gains[None], ((0, 7), (0, width - gains.shape[0])))
    s_qkv = Spread(jnp.concatenate([w_qkv, gain_rows]), axis, LEVEL)
    s_rest = Spread(jnp.concatenate([w_attn_out, spans_of(w_ff_out, width)]), axis, CROSSED)
    s_in = Spread(w_in, axis, LEVEL)
    r_ff, r_in, r_qkv = Reduce(axis, CROSSED, width), Reduce(axis, LEVEL, width), Reduce(axis, CROSSED, width)
    cosine, sine, seg_column, seg_row = tables(segment)

    s_qkv.near()
    s_qkv.nearer()
    s_qkv.block, s_rest.shard, s_in.shard, cosine, sine, seg_column, seg_row = tie(
        s_qkv.block, s_rest.shard, s_in.shard, cosine, sine, seg_column, seg_row
    )
    s_qkv.far()
    s_rest.near()
    s_in.near()
    s_rest.nearer()
    s_in.nearer()
    s_qkv.farther()
    w_qkv = s_qkv.result()
    gains = find_gains(w_qkv, rows_qkv, width)
    gain_one, gain_two = gains[:1], gains[1:]
    gain_one, s_rest.block, s_in.block = tie(gain_one, s_rest.block, s_in.block)
    s_rest.far()
    s_in.far()
    qkv, hidden_one = project(tokens, gain_one, cosine, sine, w_qkv, rows_qkv)
    done = attend(qkv, seg_column, seg_row, width, 0, pairs // 4)
    done = attend(qkv, seg_column, seg_row, width, pairs // 4, pairs // 4, done)
    done, s_rest.one, s_rest.three, s_in.one, s_in.three = tie(done, s_rest.one, s_rest.three, s_in.one, s_in.three)
    s_rest.farther()
    s_in.farther()
    done = attend(qkv, seg_column, seg_row, width, pairs // 2, pairs // 4, done)
    done = attend(qkv, seg_column, seg_row, width, 3 * pairs // 4, pairs // 4, done)
    done, s_rest.two, s_in.two = tie(done, s_rest.two, s_in.two)
    attn_out, lse = done
    w_rest, w_in = s_rest.result(), s_in.result()
    resid, hidden_two = join(tokens, attn_out, gain_two, w_rest, rows_out)
    output, mid, low, g_two, g_in, g_ff = ffn(
        resid, hidden_two, cotangent, gain_two, w_in, w_rest, units, padded, rows_out, rows_ff
    )

    rows_of = lambda grad: grad.reshape(n, -1, grad.shape[-1])
    calls = pairs
    back = lambda k, heads, before=None: attend_back(
        qkv, attn_out, heads, lse, seg_column, seg_row, cosine, sine, k * pairs // calls, pairs // calls, before
    )
    r_ff.pair((rows_of(g_ff),))
    grad_heads, g_out = join_back(low, attn_out, w_rest, rows_out)
    r_in.pair((rows_of(g_in), rows_of(g_out)))
    grad_heads, r_ff.twins = tie(grad_heads, r_ff.twins)
    r_ff.pack()
    grad_heads, r_ff.one, r_ff.two = tie(grad_heads, r_ff.one, r_ff.two)
    r_ff.far()
    some = back(1, grad_heads, back(0, grad_heads))
    some, r_in.twins, r_ff.one, r_ff.two = tie(some, r_in.twins, r_ff.one, r_ff.two)
    r_in.pack()
    r_ff.repack()
    some, r_in.one, r_in.two, r_ff.three = tie(some, r_in.one, r_in.two, r_ff.three)
    r_in.far()
    r_ff.farther()
    for k in (2, 3, 4, 5):
        some = back(k, grad_heads, some)
    some, r_in.one, r_in.two, r_ff.three = tie(some, r_in.one, r_in.two, r_ff.three)
    r_in.repack()
    r_ff.gather()
    some, r_in.three, r_ff.block = tie(some, r_in.three, r_ff.block)
    r_in.farther()
    r_ff.near()
    grad_projected = back(7, grad_heads, back(6, grad_heads, some))
    grad_projected, r_in.three, r_ff.one, r_ff.two = tie(grad_projected, r_in.three, r_ff.one, r_ff.two)
    r_in.gather()
    grad_projected, r_in.block = tie(grad_projected, r_in.block)
    r_in.near()
    r_ff.nearer()
    g_qkv = project_grad(grad_projected, hidden_one)
    r_qkv.pair((rows_of(g_qkv),))
    r_qkv.twins, r_in.one, r_in.two, r_ff.three = tie(r_qkv.twins, r_in.one, r_in.two, r_ff.three)
    r_qkv.pack()
    r_in.nearer()
    mid, r_qkv.one, r_qkv.two = tie(mid, r_qkv.one, r_qkv.two)
    r_qkv.far()
    grad_tokens, g_one = project_back(grad_projected, w_qkv, rows_qkv, tokens, mid, gain_one)
    grad_tokens, r_qkv.one, r_qkv.two, r_in.three = tie(grad_tokens, r_qkv.one, r_qkv.two, r_in.three)
    r_qkv.repack()
    r_qkv.farther()
    r_qkv.gather()
    r_qkv.near()
    r_qkv.nearer()
    rest = r_in.result()
    g_ff = r_ff.result()
    g_ff = g_ff.reshape(-1, rows_ff, width).transpose(1, 0, 2).reshape(rows_ff, -1)[:, :units]
    return output, grad_tokens, r_qkv.result(), rest[padded:], rest[:padded], g_ff, g_one, g_two


def body(tokens, cotangent, segment, w_qkv, w_attn_out, w_in, w_ff_out, norm_one, norm_two):
    axis = "fsdp"
    n = lax.axis_size(axis)
    rows_in = w_in.shape[0]
    padded = -(-rows_in // 16) * 16
    w_in = jnp.pad(w_in, ((0, padded - rows_in), (0, 0)))
    w_ff_out = jnp.pad(
        w_ff_out.reshape(-1, n // 2, rows_in), ((0, 0), (0, 0), (0, padded - rows_in))
    ).reshape(-1, n // 2 * padded)
    aligned = not any(w.shape[0] % 16 for w in (w_qkv, w_attn_out, w_ff_out))
    way = by_links if aligned and n == 2 * Z * Y * X else by_collectives
    output, grad_tokens, g_qkv, g_out, g_in, g_ff, g_one, g_two = way(
        tokens, cotangent, segment, w_qkv, w_attn_out, w_in, w_ff_out, jnp.concatenate([norm_one, norm_two]), padded, axis
    )
    g_in, g_ff, g_norms = finish(g_in, g_ff, rows_in, padded, n, axis, g_one, g_two)
    return (output, grad_tokens, g_qkv, g_out, g_in, g_ff, g_norms[0], g_norms[1])


def solution(mesh):
    rows, flat = P("fsdp", None), P("fsdp")
    return jax.shard_map(
        body,
        mesh=mesh,
        in_specs=(rows, rows, flat, rows, rows, rows, rows, flat, flat),
        out_specs=(rows, rows, rows, rows, rows, rows, flat, flat),
        check_vma=False,
    )
```

time: 1070 us -> 551 us (0.51)
  matrix products: 479 us -> 0 us
  Pallas kernels: 0 us -> 343 us
  blocking collectives: 332 us -> 0 us
  local copies, waits for them, and re-layouts: 111 us -> 22 us
  starting transfers between devices: 10.5 us -> 54.2 us
  waiting for transfers between devices: 55.7 us -> 98.9 us
  other arithmetic: 58.2 us -> 23.2 us
  between operations: 14.8 us -> 1.57 us
    dot_general x124 -> x0, matrix products: 479 us -> none  [the longest x52 207 us: matmul_nt(): lax.dot_general(left, right, (((1,), (1,)), ((), ())), preferred_element_...]
    pallas_call x0 -> x28, Pallas kernels: none -> 343 us  [the longest x6 140 us: fetching_call(): return lambda *args: made(*[order for order, _ in weights], *pieces, *args)]
    unnamed x3 -> x0, blocking collectives: 332 us -> none
    ppermute x0 -> x52, waiting for transfers between devices: none -> 98.5 us  [the longest x36 77 us: hop(): return lax.ppermute(array, axis, pairs)]
    unnamed x72 -> x53, local copies, waits for them, and re-layouts: 68.6 us -> 4.74 us
    all_gather x4 -> x0, waiting for transfers between devices: 53 us -> none  [the longest x1 32.5 us: body(): lax.all_gather(w_ff_out, 'fsdp', axis=0, tiled=True)]
    ppermute x0 -> x52, starting transfers between devices: none -> 51.6 us  [the longest x36 47.5 us: hop(): return lax.ppermute(array, axis, pairs)]
    reduce_sum x35 -> x2, other arithmetic: 30.2 us -> 0.6 us  [the longest x1 0.55 us: tables(): jnp.sum((order[None, :] < order[:, None]).astype(jnp.int32), axis=1)]
  transfers between devices with their start and end apart: 8 -> 53, of which waited for: 3 -> 14; matrix products, arithmetic and copies ran while one was open for 78% -> 6% of each run, Pallas kernels for 0% -> 40%
where the time goes in v1:
time: 551 us; the launch traced here: 543 us
  Pallas kernels  343 us (62%)
  waiting for transfers between devices  98.9 us (18%)
  starting transfers between devices  54.2 us (10%)
  other arithmetic  23.2 us (4%)
  local copies, waits for them, and re-layouts  22 us (4%)
    pallas_call x6, Pallas kernels, fetching_call(): return lambda *args: made(*[order for order, _ in weights], *pieces, *args)  140 us
    pallas_call x8, Pallas kernels, attend_back(): call(kernel, name='attend_back', grid=(number,), in_specs=[tall(0), tall(...  89.3 us
    ppermute x36, waiting for transfers between devices, hop(): return lax.ppermute(array, axis, pairs)  77 us
    pallas_call x4, Pallas kernels, attend(): call(kernel, name='attend', grid=(number,), in_specs=[tall(0), tall(pairs...  61.5 us
    ppermute x36, starting transfers between devices, hop(): return lax.ppermute(array, axis, pairs)  47.5 us
    pallas_call x9, Pallas kernels, collect(): pl.pallas_call(kernel, name='collect_grads', grid_spec=pltpu.PrefetchScal...  40.9 us
    ppermute x16, waiting for transfers between devices, swap_cores(): return lax.ppermute(array, axis, [(i, i ^ 1) for i in range(2 * Z * Y * X)])  21.5 us
    pallas_call x1, Pallas kernels, project_grad(): call(project_grad_kernel, name='grad_qkv', grid=(3 * per,), in_specs=[pl....  11.6 us
  transfers between devices with their start and end apart: 53, of which 14 were waited for; matrix products, arithmetic and copies ran while one was open for 6% of the time, Pallas kernels for 40%

profile of v1, /device:TPU:0, one launch (start us, length us, event | category | flops | bytes accessed | tf_op | source)
XLA Modules:
  0.0 543.0 jit_solution(17531994174352322249)
XLA Ops:
  16.8 5.2 collective-permute-done.1
  26.2 19.0 %collective-permute-done.3.refs_2_ = bf16[4,104,1024]{2,1,0:T(8,128)(2,1)} collective-permute-done((bf16[4,104,1024]{2,1,0:T(8,128)(2,1)S(1)}, bf16[4,104,1024]{2,1,0:T(8,128)(2,1)}, u32[]{:S(2)}, u32[]{:S(2)}) %collective-permute-start.3) | collective-permute-done | bytes 852000 | tf_op jit(solution)/shard_map/ppermute | solution.py:598
  49.0 6.3 %collective-permute-done.10 = bf16[128,1024]{1,0:T(8,128)(2,1)S(1)} collective-permute-done((bf16[128,1024]{1,0:T(8,128)(2,1)S(1)}, bf16[128,1024]{1,0:T(8,128)(2,1)S(1)}, u32[]{:S(2)}, u32[]{:S(2)}) %collective-permute-start.10) | collective-permute-done | bytes 262176 | tf_op jit(solution)/shard_map/ppermute | solution.py:598
  55.6 10.1 %collective-permute-done.12 = bf16[128,1024]{1,0:T(8,128)(2,1)S(1)} collective-permute-done((bf16[128,1024]{1,0:T(8,128)(2,1)S(1)}, bf16[128,1024]{1,0:T(8,128)(2,1)S(1)}, u32[]{:S(2)}, u32[]{:S(2)}) %collective-permute-start.12) | collective-permute-done | bytes 262176 | tf_op jit(solution)/shard_map/ppermute | solution.py:598
  67.6 8.0 %collective-permute-done.11 = bf16[128,1024]{1,0:T(8,128)(2,1)S(1)} collective-permute-done((bf16[128,1024]{1,0:T(8,128)(2,1)S(1)}, bf16[128,1024]{1,0:T(8,128)(2,1)S(1)}, u32[]{:S(2)}, u32[]{:S(2)}) %collective-permute-start.11) | collective-permute-done | bytes 262176 | tf_op jit(solution)/shard_map/ppermute | solution.py:598
  77.5 7.3 %collective-permute-done.14 = bf16[176,1024]{1,0:T(8,128)(2,1)S(1)} collective-permute-done((bf16[176,1024]{1,0:T(8,128)(2,1)S(1)}, bf16[176,1024]{1,0:T(8,128)(2,1)S(1)}, u32[]{:S(2)}, u32[]{:S(2)}) %collective-permute-start.14) | collective-permute-done | bytes 360480 | tf_op jit(solution)/shard_map/ppermute | solution.py:598
  94.3 20.0 %norm_project.1 = (bf16[1024,3072]{1,0:T(8,128)(2,1)}, bf16[1024,1024]{1,0:T(8,128)(2,1)}) custom-call(s32[32]{0:T(128)} %pad_add_fusion.2.refs_0_, bf16[4,104,1024]{2,1,0:T(8,128)(2,1)} %copy-done.3, bf16[4,104,1024]{2,1,0:T(8,128)(2,1)} %collective-permute-done.3.refs_2_, bf16[4,104,1024]{2,1,0:T(8,128)(2,1)} %collective-permute-done.4.refs_3_, ...), custom_call_target="tpu_custom_call" | custom-call | flops 6442450944 | bytes 16777216 | tf_op jit(solution)/shard_map/norm_project/pallas_call | solution.py:124
  114.4 15.4 %attend.4 = (bf16[1024,1024]{1,0:T(8,128)(2,1)}, f32[8,2,1024]{2,1,0:T(2,128)}) custom-call(bf16[1024,3072]{1,0:T(8,128)(2,1)} %get-tuple-element.101.refs_0_.refs_1_.refs_2_, bf16[1024,3072]{1,0:T(8,128)(2,1)} %get-tuple-element.101.refs_0_.refs_1_.refs_2_, bf16[1024,3072]{1,0:T(8,128)(2,1)} %get-tuple-element.101.refs_0_.refs_1_.refs_2_, ...), custom_call_target="tpu_custom_call" | custom-call | flops 4294967296 | bytes 2097152 | tf_op jit(solution)/shard_map/attend/pallas_call | solution.py:216
  129.8 15.4 %attend.5 = (bf16[1024,1024]{1,0:T(8,128)(2,1)}, f32[8,2,1024]{2,1,0:T(2,128)}) custom-call(bf16[1024,3072]{1,0:T(8,128)(2,1)} %get-tuple-element.101.refs_0_.refs_1_.refs_2_, bf16[1024,3072]{1,0:T(8,128)(2,1)} %get-tuple-element.101.refs_0_.refs_1_.refs_2_, ...), custom_call_target="tpu_custom_call", output_to_operand_aliasing={{0}: (5, {}), {1}: (6, {})} | custom-call | flops 4294967296 | bytes 2097152 | tf_op jit(solution)/shard_map/attend/pallas_call | solution.py:216
  147.8 15.4 %attend.6 = (bf16[1024,1024]{1,0:T(8,128)(2,1)}, f32[8,2,1024]{2,1,0:T(2,128)}) custom-call(bf16[1024,3072]{1,0:T(8,128)(2,1)} %get-tuple-element.101.refs_0_.refs_1_.refs_2_, bf16[1024,3072]{1,0:T(8,128)(2,1)} %get-tuple-element.101.refs_0_.refs_1_.refs_2_, ...), custom_call_target="tpu_custom_call", output_to_operand_aliasing={{0}: (5, {}), {1}: (6, {})} | custom-call | flops 4294967296 | bytes 2097152 | tf_op jit(solution)/shard_map/attend/pallas_call | solution.py:216
  163.2 15.4 %attend.7 = (bf16[1024,1024]{1,0:T(8,128)(2,1)}, f32[8,2,1024]{2,1,0:T(2,128)}) custom-call(bf16[1024,3072]{1,0:T(8,128)(2,1)} %get-tuple-element.101.refs_0_.refs_1_.refs_2_, bf16[1024,3072]{1,0:T(8,128)(2,1)} %get-tuple-element.101.refs_0_.refs_1_.refs_2_, ...), custom_call_target="tpu_custom_call", output_to_operand_aliasing={{0}: (5, {}), {1}: (6, {})} | custom-call | flops 4294967296 | bytes 2097152 | tf_op jit(solution)/shard_map/attend/pallas_call | solution.py:216
  180.7 5.6 %collective-permute-done.28.refs_7_.refs_16_ = bf16[4,128,1024]{2,1,0:T(8,128)(2,1)S(1)} collective-permute-done((bf16[4,128,1024]{2,1,0:T(8,128)(2,1)}, bf16[4,128,1024]{2,1,0:T(8,128)(2,1)S(1)}, u32[]{:S(2)}, u32[]{:S(2)}) %collective-permute-start.28) | collective-permute-done | bytes 1048608 | tf_op jit(solution)/shard_map/ppermute | solution.py:602
  187.4 8.9 %attn_out_norm.1 = (f32[1024,1024]{1,0:T(8,128)}, bf16[1024,1024]{1,0:T(8,128)(2,1)}) custom-call(s32[32]{0:T(128)} %pad_add_fusion.3.refs_0_.refs_1_, bf16[4,128,1024]{2,1,0:T(8,128)(2,1)} %copy-done.2, bf16[4,128,1024]{2,1,0:T(8,128)(2,1)} %collective-permute-done.16.refs_2_.refs_11_, bf16[4,128,1024]{2,1,0:T(8,128)(2,1)} %collective-permute-done.20.refs_3_.refs_12_, ...), custom_call_target="tpu_custom_call" | custom-call | flops 2147483648 | bytes 12582912 | tf_op jit(solution)/shard_map/attn_out_norm/pallas_call | solution.py:124
  196.3 77.3 %ffn_forward_backward.1 = (bf16[1024,1024]{1,0:T(8,128)(2,1)}, f32[1024,1024]{1,0:T(8,128)}, bf16[1024,1024]{1,0:T(8,128)(2,1)}, f32[1,1024]{1,0:T(1,128)}, bf16...) custom-call(s32[32]{0:T(128)} %pad_add_fusion.2.refs_0_, s32[32]{0:T(128)} %pad_add_fusion.3.refs_0_.refs_1_, ...), custom_call_target="tpu_custom_call" | custom-call | flops 53150220288 | bytes 55574528 | tf_op jit(solution)/shard_map/ffn_forward_backward/pallas_call | solution.py:124
  274.3 10.7 %attn_out_back.1 = (bf16[1024,1024]{1,0:T(8,128)(2,1)}, bf16[1024,1024]{1,0:T(8,128)(2,1)}) custom-call(s32[32]{0:T(128)} %pad_add_fusion.3.refs_0_.refs_1_, bf16[4,128,1024]{2,1,0:T(8,128)(2,1)} %copy-done.2, bf16[4,128,1024]{2,1,0:T(8,128)(2,1)} %collective-permute-done.16.refs_2_.refs_11_, bf16[4,128,1024]{2,1,0:T(8,128)(2,1)} %collective-permute-done.20.refs_3_.refs_12_, ...), custom_call_target="tpu_custom_call" | custom-call | flops 4294967296 | bytes 10485760 | tf_op jit(solution)/shard_map/attn_out_back/pallas_call | solution.py:124
  287.1 15.9 %collective-permute-done.30.refs_4_.refs_5_.refs_6_.refs_7_ = bf16[32,32,2816]{2,1,0:T(8,128)(2,1)} collective-permute-done((bf16[32,32,2816]{2,1,0:T(8,128)(2,1)}, bf16[32,32,2816]{2,1,0:T(8,128)(2,1)}, u32[]{:S(2)}, u32[]{:S(2)}) %collective-permute-start.30) | collective-permute-done | bytes 5767200 | tf_op jit(solution)/shard_map/ppermute | solution.py:602
  309.3 11.1 %attend_back.8.refs_10_ = bf16[3,1024,1024]{2,1,0:T(8,128)(2,1)} custom-call(bf16[1024,3072]{1,0:T(8,128)(2,1)} %get-tuple-element.101.refs_0_.refs_1_.refs_2_, bf16[1024,3072]{1,0:T(8,128)(2,1)} %get-tuple-element.101.refs_0_.refs_1_.refs_2_, bf16[1024,3072]{1,0:T(8,128)(2,1)} %get-tuple-element.101.refs_0_.refs_1_.refs_2_, ...), custom_call_target="tpu_custom_call" | custom-call | flops 5368709120 | bytes 2097152 | tf_op jit(solution)/shard_map/attend_back/pallas_call | solution.py:287
  320.4 11.1 %attend_back.9.refs_10_ = bf16[3,1024,1024]{2,1,0:T(8,128)(2,1)} custom-call(bf16[1024,3072]{1,0:T(8,128)(2,1)} %get-tuple-element.101.refs_0_.refs_1_.refs_2_, bf16[1024,3072]{1,0:T(8,128)(2,1)} %get-tuple-element.101.refs_0_.refs_1_.refs_2_, bf16[1024,3072]{1,0:T(8,128)(2,1)} %get-tuple-element.101.refs_0_.refs_1_.refs_2_, ...), custom_call_target="tpu_custom_call", output_to_operand_aliasing={{}: (10, {})} | custom-call | flops 5368709120 | bytes 2097152 | tf_op jit(solution)/shard_map/attend_back/pallas_call | solution.py:287
  336.0 6.0 %collect_grads.10 = (bf16[4,208,1024]{2,1,0:T(8,128)(2,1)}, bf16[4,208,1024]{2,1,0:T(8,128)(2,1)}) custom-call(s32[4,4]{1,0:T(4,128)} %pad_add_fusion.1.chosen_ref, bf16[32,176,1024]{2,1,0:T(8,128)(2,1)} %bitcast.150, bf16[32,176,1024]{2,1,0:T(8,128)(2,1)} %bitcast.151, bf16[32,176,1024]{2,1,0:T(8,128)(2,1)} %bitcast.152, bf16[32,176,1024]{2,1,0:T(8,128)(2,1)} %bitcast.153, ...), custom_call_target="tpu_custom_call" | custom-call | flops 1703936 | bytes 10223616 | tf_op jit(solution)/shard_map/collect_grads/pallas_call | solution.py:699
  344.1 11.2 %attend_back.10.refs_10_ = bf16[3,1024,1024]{2,1,0:T(8,128)(2,1)} custom-call(bf16[1024,3072]{1,0:T(8,128)(2,1)} %get-tuple-element.101.refs_0_.refs_1_.refs_2_, bf16[1024,3072]{1,0:T(8,128)(2,1)} %get-tuple-element.101.refs_0_.refs_1_.refs_2_, bf16[1024,3072]{1,0:T(8,128)(2,1)} %get-tuple-element.101.refs_0_.refs_1_.refs_2_, ...), custom_call_target="tpu_custom_call", output_to_operand_aliasing={{}: (10, {})} | custom-call | flops 5368709120 | bytes 2097152 | tf_op jit(solution)/shard_map/attend_back/pallas_call | solution.py:287
  355.7 11.2 %attend_back.11.refs_10_ = bf16[3,1024,1024]{2,1,0:T(8,128)(2,1)} custom-call(bf16[1024,3072]{1,0:T(8,128)(2,1)} %get-tuple-element.101.refs_0_.refs_1_.refs_2_, bf16[1024,3072]{1,0:T(8,128)(2,1)} %get-tuple-element.101.refs_0_.refs_1_.refs_2_, bf16[1024,3072]{1,0:T(8,128)(2,1)} %get-tuple-element.101.refs_0_.refs_1_.refs_2_, ...), custom_call_target="tpu_custom_call", output_to_operand_aliasing={{}: (10, {})} | custom-call | flops 5368709120 | bytes 2097152 | tf_op jit(solution)/shard_map/attend_back/pallas_call | solution.py:287
  366.9 11.1 %attend_back.12.refs_10_ = bf16[3,1024,1024]{2,1,0:T(8,128)(2,1)} custom-call(bf16[1024,3072]{1,0:T(8,128)(2,1)} %get-tuple-element.101.refs_0_.refs_1_.refs_2_, bf16[1024,3072]{1,0:T(8,128)(2,1)} %get-tuple-element.101.refs_0_.refs_1_.refs_2_, bf16[1024,3072]{1,0:T(8,128)(2,1)} %get-tuple-element.101.refs_0_.refs_1_.refs_2_, ...), custom_call_target="tpu_custom_call", output_to_operand_aliasing={{}: (10, {})} | custom-call | flops 5368709120 | bytes 2097152 | tf_op jit(solution)/shard_map/attend_back/pallas_call | solution.py:287
  378.1 11.2 %attend_back.13.refs_10_ = bf16[3,1024,1024]{2,1,0:T(8,128)(2,1)} custom-call(bf16[1024,3072]{1,0:T(8,128)(2,1)} %get-tuple-element.101.refs_0_.refs_1_.refs_2_, bf16[1024,3072]{1,0:T(8,128)(2,1)} %get-tuple-element.101.refs_0_.refs_1_.refs_2_, bf16[1024,3072]{1,0:T(8,128)(2,1)} %get-tuple-element.101.refs_0_.refs_1_.refs_2_, ...), custom_call_target="tpu_custom_call", output_to_operand_aliasing={{}: (10, {})} | custom-call | flops 5368709120 | bytes 2097152 | tf_op jit(solution)/shard_map/attend_back/pallas_call | solution.py:287
  390.4 5.0 collect_grads.12
  405.5 11.1 %attend_back.14.refs_10_ = bf16[3,1024,1024]{2,1,0:T(8,128)(2,1)} custom-call(bf16[1024,3072]{1,0:T(8,128)(2,1)} %get-tuple-element.101.refs_0_.refs_1_.refs_2_, bf16[1024,3072]{1,0:T(8,128)(2,1)} %get-tuple-element.101.refs_0_.refs_1_.refs_2_, bf16[1024,3072]{1,0:T(8,128)(2,1)} %get-tuple-element.101.refs_0_.refs_1_.refs_2_, ...), custom_call_target="tpu_custom_call", output_to_operand_aliasing={{}: (10, {})} | custom-call | flops 5368709120 | bytes 2097152 | tf_op jit(solution)/shard_map/attend_back/pallas_call | solution.py:287
  416.6 11.2 %attend_back.15.gp_ref.refs_9_ = bf16[3,1024,1024]{2,1,0:T(8,128)(2,1)} custom-call(bf16[1024,3072]{1,0:T(8,128)(2,1)} %get-tuple-element.101.refs_0_.refs_1_.refs_2_, bf16[1024,3072]{1,0:T(8,128)(2,1)} %get-tuple-element.101.refs_0_.refs_1_.refs_2_, bf16[1024,3072]{1,0:T(8,128)(2,1)} %get-tuple-element.101.refs_0_.refs_1_.refs_2_, ...), custom_call_target="tpu_custom_call", output_to_operand_aliasing={{}: (10, {})} | custom-call | flops 5368709120 | bytes 2097152 | tf_op jit(solution)/shard_map/attend_back/pallas_call | solution.py:287
  429.1 6.2 %collect_grads.14 = f32[4,208,1024]{2,1,0:T(8,128)} custom-call(s32[4,4]{1,0:T(4,128)} %pad_add_fusion.1.chosen_ref, bf16[32,176,1024]{2,1,0:T(8,128)(2,1)} %bitcast.158, bf16[32,176,1024]{2,1,0:T(8,128)(2,1)} %bitcast.159, bf16[32,176,1024]{2,1,0:T(8,128)(2,1)} %bitcast.160, bf16[32,176,1024]{2,1,0:T(8,128)(2,1)} %bitcast.161, ...), custom_call_target="tpu_custom_call" | custom-call | flops 2555904 | bytes 8519680 | tf_op jit(solution)/shard_map/collect_grads/pallas_call | solution.py:699
  435.4 11.6 %grad_qkv.1 = bf16[3072,1024]{1,0:T(8,128)(2,1)} custom-call(bf16[3,1024,1024]{2,1,0:T(8,128)(2,1)} %attend_back.15.gp_ref.refs_9_, bf16[1024,1024]{1,0:T(8,128)(2,1)} %get-tuple-element.160.hid_ref), custom_call_target="tpu_custom_call" | custom-call | flops 6442450944 | bytes 14680064 | tf_op jit(solution)/shard_map/grad_qkv/pallas_call | solution.py:492
  455.4 16.3 %collective-permute-done.44 = bf16[96,1024]{1,0:T(8,128)(2,1)} collective-permute-done((bf16[96,1024]{1,0:T(8,128)(2,1)}, bf16[96,1024]{1,0:T(8,128)(2,1)}, u32[]{:S(2)}, u32[]{:S(2)}) %collective-permute-start.44) | collective-permute-done | bytes 196640 | tf_op jit(solution)/shard_map/ppermute | solution.py:598
  483.6 20.1 %grad_tokens.1 = (f32[1024,1024]{1,0:T(8,128)}, f32[1,1024]{1,0:T(1,128)}) custom-call(s32[32]{0:T(128)} %pad_add_fusion.2.refs_0_, bf16[4,104,1024]{2,1,0:T(8,128)(2,1)} %copy-done.3, bf16[4,104,1024]{2,1,0:T(8,128)(2,1)} %collective-permute-done.3.refs_2_, bf16[4,104,1024]{2,1,0:T(8,128)(2,1)} %collective-permute-done.4.refs_3_, ...), custom_call_target="tpu_custom_call" | custom-call | flops 6442450944 | bytes 25165824 | tf_op jit(solution)/shard_map/grad_tokens/pallas_call | solution.py:124
  520.3 4.3 collect_grads.17
  533.3 4.4 collective-permute-start.51
  (213 shorter events, 122.2 us)
Async XLA Ops:
  23.2 22.0 %collective-permute-start.3 = (bf16[4,104,1024]{2,1,0:T(8,128)(2,1)S(1)}, bf16[4,104,1024]{2,1,0:T(8,128)(2,1)}, u32[]{:S(2)}, u32[]{:S(2)}) collective-permute-start(bf16[4,104,1024]{2,1,0:T(8,128)(2,1)S(1)} %pad_maximum_fusion.2.refs_1_), channel_id=1, source_target_pairs={{0,4},{1,3},{2,6},{3,1},{4,0},{5,7},{6,2},{7,5},{8,12},{9,11},{10,... | collective-permute-start | bytes 2555912 | tf_op jit(solution)/shard_map/ppermute | solution.py:598
  24.7 42.1 %collective-permute-start.5 = (bf16[4,104,1024]{2,1,0:T(8,128)(2,1)S(1)}, bf16[4,104,1024]{2,1,0:T(8,128)(2,1)}, u32[]{:S(2)}, u32[]{:S(2)}) collective-permute-start(bf16[4,104,1024]{2,1,0:T(8,128)(2,1)S(1)} %pad_maximum_fusion.2.refs_1_), channel_id=1, source_target_pairs={{0,2},{1,5},{2,0},{3,7},{4,6},{5,1},{6,4},{7,3},{8,10},{9,13},{10,... | collective-permute-start | bytes 2555912 | tf_op jit(solution)/shard_map/ppermute | solution.py:598
  45.2 21.7 %collective-permute-start.4 = (bf16[4,104,1024]{2,1,0:T(8,128)(2,1)}, bf16[4,104,1024]{2,1,0:T(8,128)(2,1)}, u32[]{:S(2)}, u32[]{:S(2)}) collective-permute-start(bf16[4,104,1024]{2,1,0:T(8,128)(2,1)} %collective-permute-done.3.refs_2_), channel_id=1, source_target_pairs={{0,2},{1,5},{2,0},{3,7},{4,6},{5,1},{6,4},{7,3},{8,10},{9,13},{10,... | collective-permute-start | bytes 2555912 | tf_op jit(solution)/shard_map/ppermute | solution.py:598
  45.2 21.1 %collective-permute-start.13 = (bf16[176,1024]{1,0:T(8,128)(2,1)S(1)}, bf16[176,1024]{1,0:T(8,128)(2,1)S(1)}, u32[]{:S(2)}, u32[]{:S(2)}) collective-permute-start(bf16[176,1024]{1,0:T(8,128)(2,1)S(1)} %pad.19), channel_id=1, source_target_pairs={{0,8},{1,9},{2,10},{3,11},{4,12},{5,13},{6,14},{7,15},{8,16},{9,17... | collective-permute-start | bytes 1081352 | tf_op jit(solution)/shard_map/ppermute | solution.py:598
  66.3 19.9 %collective-permute-start.6 = (bf16[4,104,1024]{2,1,0:T(8,128)(2,1)S(1)}, bf16[4,104,1024]{2,1,0:T(8,128)(2,1)}, u32[]{:S(2)}, u32[]{:S(2)}) collective-permute-start(bf16[4,104,1024]{2,1,0:T(8,128)(2,1)S(1)} %pad_maximum_fusion.2.refs_1_), channel_id=1, source_target_pairs={{0,1},{1,0},{2,3},{3,2},{4,5},{5,4},{6,7},{7,6},{8,9},{9,8},{10,11... | collective-permute-start | bytes 2555912 | tf_op jit(solution)/shard_map/ppermute | solution.py:602
  90.1 55.0 %collective-permute-start.18 = (bf16[4,176,1024]{2,1,0:T(8,128)(2,1)S(1)}, bf16[4,176,1024]{2,1,0:T(8,128)(2,1)}, u32[]{:S(2)}, u32[]{:S(2)}) collective-permute-start(bf16[4,176,1024]{2,1,0:T(8,128)(2,1)S(1)} %pad_maximum_fusion.refs_2_), channel_id=1, source_target_pairs={{0,4},{1,3},{2,6},{3,1},{4,0},{5,7},{6,2},{7,5},{8,12},{9,11},{10,... | collective-permute-start | bytes 4325384 | tf_op jit(solution)/shard_map/ppermute | solution.py:598
  90.4 54.8 %collective-permute-start.19 = (bf16[4,176,1024]{2,1,0:T(8,128)(2,1)S(1)}, bf16[4,176,1024]{2,1,0:T(8,128)(2,1)}, u32[]{:S(2)}, u32[]{:S(2)}) collective-permute-start(bf16[4,176,1024]{2,1,0:T(8,128)(2,1)S(1)} %pad_maximum_fusion.refs_2_), channel_id=1, source_target_pairs={{0,2},{1,5},{2,0},{3,7},{4,6},{5,1},{6,4},{7,3},{8,10},{9,13},{10,... | collective-permute-start | bytes 4325384 | tf_op jit(solution)/shard_map/ppermute | solution.py:598
  90.9 54.3 %collective-permute-start.16 = (bf16[4,128,1024]{2,1,0:T(8,128)(2,1)S(1)}, bf16[4,128,1024]{2,1,0:T(8,128)(2,1)}, u32[]{:S(2)}, u32[]{:S(2)}) collective-permute-start(bf16[4,128,1024]{2,1,0:T(8,128)(2,1)S(1)} %pad_maximum_fusion.1.refs_1_.refs_10_), channel_id=1, source_target_pairs={{0,4},{1,9},{2,6},{3,11},{4,0},{5,13},{6,2},{7,15},{8,12},{9,17},{... | collective-permute-start | bytes 3145736 | tf_op jit(solution)/shard_map/ppermute | solution.py:598
  92.6 52.5 %collective-permute-start.17 = (bf16[4,128,1024]{2,1,0:T(8,128)(2,1)S(1)}, bf16[4,128,1024]{2,1,0:T(8,128)(2,1)}, u32[]{:S(2)}, u32[]{:S(2)}) collective-permute-start(bf16[4,128,1024]{2,1,0:T(8,128)(2,1)S(1)} %pad_maximum_fusion.1.refs_1_.refs_10_), channel_id=1, source_target_pairs={{0,2},{1,25},{2,0},{3,27},{4,6},{5,29},{6,4},{7,31},{8,10},{9,1},{... | collective-permute-start | bytes 3145736 | tf_op jit(solution)/shard_map/ppermute | solution.py:598
  145.2 33.9 %collective-permute-start.21 = (bf16[4,176,1024]{2,1,0:T(8,128)(2,1)}, bf16[4,176,1024]{2,1,0:T(8,128)(2,1)}, u32[]{:S(2)}, u32[]{:S(2)}) collective-permute-start(bf16[4,176,1024]{2,1,0:T(8,128)(2,1)} %collective-permute-done.18.refs_3_), channel_id=1, source_target_pairs={{0,2},{1,5},{2,0},{3,7},{4,6},{5,1},{6,4},{7,3},{8,10},{9,13},{10,... | collective-permute-start | bytes 4325384 | tf_op jit(solution)/shard_map/ppermute | solution.py:598
  145.7 32.8 %collective-permute-start.20 = (bf16[4,128,1024]{2,1,0:T(8,128)(2,1)}, bf16[4,128,1024]{2,1,0:T(8,128)(2,1)}, u32[]{:S(2)}, u32[]{:S(2)}) collective-permute-start(bf16[4,128,1024]{2,1,0:T(8,128)(2,1)} %collective-permute-done.16.refs_2_.refs_11_), channel_id=1, source_target_pairs={{0,2},{1,9},{2,0},{3,11},{4,6},{5,13},{6,4},{7,15},{8,10},{9,17},{... | collective-permute-start | bytes 3145736 | tf_op jit(solution)/shard_map/ppermute | solution.py:598
  147.3 31.9 %collective-permute-start.26 = (bf16[4,128,1024]{2,1,0:T(8,128)(2,1)S(1)}, bf16[4,128,1024]{2,1,0:T(8,128)(2,1)}, u32[]{:S(2)}, u32[]{:S(2)}) collective-permute-start(bf16[4,128,1024]{2,1,0:T(8,128)(2,1)S(1)} %pad_maximum_fusion.1.refs_1_.refs_10_), channel_id=1, source_target_pairs={{0,1},{1,0},{2,3},{3,2},{4,5},{5,4},{6,7},{7,6},{8,9},{9,8},{10,11... | collective-permute-start | bytes 3145736 | tf_op jit(solution)/shard_map/ppermute | solution.py:602
  147.3 32.3 %collective-permute-start.27 = (bf16[4,128,1024]{2,1,0:T(8,128)(2,1)}, bf16[4,128,1024]{2,1,0:T(8,128)(2,1)}, u32[]{:S(2)}, u32[]{:S(2)}) collective-permute-start(bf16[4,128,1024]{2,1,0:T(8,128)(2,1)} %collective-permute-done.16.refs_2_.refs_11_), channel_id=1, source_target_pairs={{0,1},{1,0},{2,3},{3,2},{4,5},{5,4},{6,7},{7,6},{8,9},{9,8},{10,11... | collective-permute-start | bytes 3145736 | tf_op jit(solution)/shard_map/ppermute | solution.py:602
  147.8 31.9 %collective-permute-start.29 = (bf16[4,128,1024]{2,1,0:T(8,128)(2,1)}, bf16[4,128,1024]{2,1,0:T(8,128)(2,1)}, u32[]{:S(2)}, u32[]{:S(2)}) collective-permute-start(bf16[4,128,1024]{2,1,0:T(8,128)(2,1)} %collective-permute-done.17.refs_4_.refs_13_), channel_id=1, source_target_pairs={{0,1},{1,0},{2,3},{3,2},{4,5},{5,4},{6,7},{7,6},{8,9},{9,8},{10,11... | collective-permute-start | bytes 3145736 | tf_op jit(solution)/shard_map/ppermute | solution.py:602
  273.7 57.9 %collective-permute-start.31 = (bf16[32,176,1024]{2,1,0:T(8,128)(2,1)}, bf16[32,176,1024]{2,1,0:T(8,128)(2,1)}, u32[]{:S(2)}, u32[]{:S(2)}) collective-permute-start(bf16[32,176,1024]{2,1,0:T(8,128)(2,1)} %bitcast.149), channel_id=1, source_target_pairs={{0,1},{1,0},{2,3},{3,2},{4,5},{5,4},{6,7},{7,6},{8,9},{9,8},{10,11... | collective-permute-start | bytes 34603016 | tf_op jit(solution)/shard_map/ppermute | solution.py:602
  274.1 28.9 %collective-permute-start.30 = (bf16[32,32,2816]{2,1,0:T(8,128)(2,1)}, bf16[32,32,2816]{2,1,0:T(8,128)(2,1)}, u32[]{:S(2)}, u32[]{:S(2)}) collective-permute-start(bf16[32,32,2816]{2,1,0:T(8,128)(2,1)} %bitcast.175), channel_id=1, source_target_pairs={{0,1},{1,0},{2,3},{3,2},{4,5},{5,4},{6,7},{7,6},{8,9},{9,8},{10,11... | collective-permute-start | bytes 17301512 | tf_op jit(solution)/shard_map/ppermute | solution.py:602
  285.0 46.6 %collective-permute-start.32 = (bf16[32,32,1024]{2,1,0:T(8,128)(2,1)}, bf16[32,32,1024]{2,1,0:T(8,128)(2,1)S(1)}, u32[]{:S(2)}, u32[]{:S(2)}) collective-permute-start(bf16[32,32,1024]{2,1,0:T(8,128)(2,1)} %bitcast.188), channel_id=1, source_target_pairs={{0,1},{1,0},{2,3},{3,2},{4,5},{5,4},{6,7},{7,6},{8,9},{9,8},{10,11... | collective-permute-start | bytes 6291464 | tf_op jit(solution)/shard_map/ppermute | solution.py:602
  306.9 24.7 %collective-permute-start.33 = (bf16[4,96,1024]{2,1,0:T(8,128)(2,1)}, bf16[4,96,1024]{2,1,0:T(8,128)(2,1)S(1)}, u32[]{:S(2)}, u32[]{:S(2)}) collective-permute-start(bf16[4,96,1024]{2,1,0:T(8,128)(2,1)} %get-tuple-element.136), channel_id=1, source_target_pairs={{0,2},{1,25},{2,0},{3,27},{4,6},{5,29},{6,4},{7,31},{8,10},{9,1},{... | collective-permute-start | bytes 2359304 | tf_op jit(solution)/shard_map/ppermute | solution.py:598
  307.4 24.2 %collective-permute-start.34 = (bf16[4,96,1024]{2,1,0:T(8,128)(2,1)}, bf16[4,96,1024]{2,1,0:T(8,128)(2,1)S(1)}, u32[]{:S(2)}, u32[]{:S(2)}) collective-permute-start(bf16[4,96,1024]{2,1,0:T(8,128)(2,1)} %get-tuple-element.137), channel_id=1, source_target_pairs={{0,2},{1,9},{2,0},{3,11},{4,6},{5,13},{6,4},{7,15},{8,10},{9,17},{... | collective-permute-start | bytes 2359304 | tf_op jit(solution)/shard_map/ppermute | solution.py:598
  342.0 47.3 %collective-permute-start.35 = (bf16[4,208,1024]{2,1,0:T(8,128)(2,1)}, bf16[4,208,1024]{2,1,0:T(8,128)(2,1)S(1)}, u32[]{:S(2)}, u32[]{:S(2)}) collective-permute-start(bf16[4,208,1024]{2,1,0:T(8,128)(2,1)} %get-tuple-element.145), channel_id=1, source_target_pairs={{0,2},{1,5},{2,0},{3,7},{4,6},{5,1},{6,4},{7,3},{8,10},{9,13},{10,... | collective-permute-start | bytes 5111816 | tf_op jit(solution)/shard_map/ppermute | solution.py:598
  342.5 46.7 %collective-permute-start.36 = (bf16[4,208,1024]{2,1,0:T(8,128)(2,1)}, bf16[4,208,1024]{2,1,0:T(8,128)(2,1)S(1)}, u32[]{:S(2)}, u32[]{:S(2)}) collective-permute-start(bf16[4,208,1024]{2,1,0:T(8,128)(2,1)} %get-tuple-element.146), channel_id=1, source_target_pairs={{0,2},{1,5},{2,0},{3,7},{4,6},{5,1},{6,4},{7,3},{8,10},{9,13},{10,... | collective-permute-start | bytes 5111816 | tf_op jit(solution)/shard_map/ppermute | solution.py:598
  355.3 33.9 %collective-permute-start.37 = (bf16[4,96,1024]{2,1,0:T(8,128)(2,1)}, bf16[4,96,1024]{2,1,0:T(8,128)(2,1)}, u32[]{:S(2)}, u32[]{:S(2)}) collective-permute-start(bf16[4,96,1024]{2,1,0:T(8,128)(2,1)} %collect_grads.11), channel_id=1, source_target_pairs={{0,4},{1,25},{2,6},{3,27},{4,0},{5,29},{6,2},{7,31},{8,12},{9,1},{... | collective-permute-start | bytes 2359304 | tf_op jit(solution)/shard_map/ppermute | solution.py:598
  399.7 28.2 %collective-permute-start.38 = (bf16[4,208,1024]{2,1,0:T(8,128)(2,1)S(1)}, bf16[4,208,1024]{2,1,0:T(8,128)(2,1)S(1)}, u32[]{:S(2)}, u32[]{:S(2)}) collective-permute-start(bf16[4,208,1024]{2,1,0:T(8,128)(2,1)S(1)} %copy-done.4), channel_id=1, source_target_pairs={{0,4},{1,3},{2,6},{3,1},{4,0},{5,7},{6,2},{7,5},{8,12},{9,11},{10,... | collective-permute-start | bytes 5111816 | tf_op jit(solution)/shard_map/ppermute | solution.py:598
  403.3 24.6 %collective-permute-start.39 = (bf16[96,1024]{1,0:T(8,128)(2,1)}, bf16[96,1024]{1,0:T(8,128)(2,1)S(1)}, u32[]{:S(2)}, u32[]{:S(2)}) collective-permute-start(bf16[96,1024]{1,0:T(8,128)(2,1)} %get-tuple-element.193), channel_id=1, source_target_pairs={{0,24},{1,5},{2,26},{3,7},{4,28},{5,1},{6,30},{7,3},{8,0},{9,13},{... | collective-permute-start | bytes 589832 | tf_op jit(solution)/shard_map/ppermute | solution.py:598
  403.3 24.6 %collective-permute-start.40 = (bf16[96,1024]{1,0:T(8,128)(2,1)S(1)}, bf16[96,1024]{1,0:T(8,128)(2,1)}, u32[]{:S(2)}, u32[]{:S(2)}) collective-permute-start(bf16[96,1024]{1,0:T(8,128)(2,1)S(1)} %get-tuple-element.192), channel_id=1, source_target_pairs={{0,8},{1,5},{2,10},{3,7},{4,12},{5,1},{6,14},{7,3},{8,16},{9,13},{... | collective-permute-start | bytes 589832 | tf_op jit(solution)/shard_map/ppermute | solution.py:598
  446.9 24.8 %collective-permute-start.41 = (bf16[32,96,1024]{2,1,0:T(8,128)(2,1)}, bf16[32,96,1024]{2,1,0:T(8,128)(2,1)}, u32[]{:S(2)}, u32[]{:S(2)}) collective-permute-start(bf16[32,96,1024]{2,1,0:T(8,128)(2,1)} %bitcast.162), channel_id=1, source_target_pairs={{0,1},{1,0},{2,3},{3,2},{4,5},{5,4},{6,7},{7,6},{8,9},{9,8},{10,11... | collective-permute-start | bytes 18874376 | tf_op jit(solution)/shard_map/ppermute | solution.py:602
  448.0 23.8 %collective-permute-start.42 = (bf16[208,1024]{1,0:T(8,128)(2,1)}, bf16[208,1024]{1,0:T(8,128)(2,1)}, u32[]{:S(2)}, u32[]{:S(2)}) collective-permute-start(bf16[208,1024]{1,0:T(8,128)(2,1)} %get-tuple-element.189), channel_id=1, source_target_pairs={{0,24},{1,25},{2,26},{3,27},{4,28},{5,29},{6,30},{7,31},{8,0},{9,1... | collective-permute-start | bytes 1277960 | tf_op jit(solution)/shard_map/ppermute | solution.py:598
  449.8 22.0 %collective-permute-start.43 = (bf16[208,1024]{1,0:T(8,128)(2,1)}, bf16[208,1024]{1,0:T(8,128)(2,1)}, u32[]{:S(2)}, u32[]{:S(2)}) collective-permute-start(bf16[208,1024]{1,0:T(8,128)(2,1)} %get-tuple-element.188), channel_id=1, source_target_pairs={{0,8},{1,9},{2,10},{3,11},{4,12},{5,13},{6,14},{7,15},{8,16},{9,17... | collective-permute-start | bytes 1277960 | tf_op jit(solution)/shard_map/ppermute | solution.py:598
  451.8 19.9 %collective-permute-start.44 = (bf16[96,1024]{1,0:T(8,128)(2,1)}, bf16[96,1024]{1,0:T(8,128)(2,1)}, u32[]{:S(2)}, u32[]{:S(2)}) collective-permute-start(bf16[96,1024]{1,0:T(8,128)(2,1)} %fusion.8), channel_id=1, source_target_pairs={{0,24},{1,3},{2,26},{3,1},{4,28},{5,7},{6,30},{7,5},{8,0},{9,11},{... | collective-permute-start | bytes 589832 | tf_op jit(solution)/shard_map/ppermute | solution.py:598
  475.8 27.9 %collective-permute-start.45 = (bf16[4,96,1024]{2,1,0:T(8,128)(2,1)}, bf16[4,96,1024]{2,1,0:T(8,128)(2,1)}, u32[]{:S(2)}, u32[]{:S(2)}) collective-permute-start(bf16[4,96,1024]{2,1,0:T(8,128)(2,1)} %get-tuple-element.168), channel_id=1, source_target_pairs={{0,2},{1,25},{2,0},{3,27},{4,6},{5,29},{6,4},{7,31},{8,10},{9,1},{... | collective-permute-start | bytes 2359304 | tf_op jit(solution)/shard_map/ppermute | solution.py:598
  476.3 27.4 %collective-permute-start.46 = (bf16[4,96,1024]{2,1,0:T(8,128)(2,1)}, bf16[4,96,1024]{2,1,0:T(8,128)(2,1)}, u32[]{:S(2)}, u32[]{:S(2)}) collective-permute-start(bf16[4,96,1024]{2,1,0:T(8,128)(2,1)} %get-tuple-element.169), channel_id=1, source_target_pairs={{0,2},{1,9},{2,0},{3,11},{4,6},{5,13},{6,4},{7,15},{8,10},{9,17},{... | collective-permute-start | bytes 2359304 | tf_op jit(solution)/shard_map/ppermute | solution.py:598
  479.7 24.0 %collective-permute-start.47 = (bf16[208,1024]{1,0:T(8,128)(2,1)}, bf16[208,1024]{1,0:T(8,128)(2,1)S(1)}, u32[]{:S(2)}, u32[]{:S(2)}) collective-permute-start(bf16[208,1024]{1,0:T(8,128)(2,1)} %fusion.1), channel_id=1, source_target_pairs={{0,24},{1,25},{2,26},{3,27},{4,28},{5,29},{6,30},{7,31},{8,0},{9,1... | collective-permute-start | bytes 1277960 | tf_op jit(solution)/shard_map/ppermute | solution.py:598
  (47 other events, 698.9 us)
